TPU v7x, 512 devices: a whole 4x4x16 slice. The times are simulated.
512 devices in a mesh: sta: 32 (over z_lo, y), src: 16 (over z_hi, x, core).
Axes of the slice: x: 4, y: 4, z: 16 (z_hi: 2, z_lo: 8; z = z_hi * 8 + z_lo), core: 2. Of those that a mesh axis runs over, the one named last changes fastest.
Arguments:
- green_real: bfloat16 [4096, 32768], P('sta', 'src'), may hold values from -0.2541165 to 0.2541165
- green_imag: bfloat16 [4096, 32768], P('sta', 'src'), may hold values from -0.2541165 to 0.2541165
- station_vec: float32 [2, 32, 4096], P(None, 'src', 'sta'), may hold values from -6 to 6
- source_vec: float32 [2, 32, 32768], P(None, 'sta', 'src'), may hold values from -6 to 6
- search_dir: float32 [2, 32, 32768], P(None, 'sta', 'src'), may hold values from -6 to 6
- solution: float32 [2, 32, 32768], P(None, 'sta', 'src'), may hold values from -6 to 6
- alpha_now: float32 [32], replicated, may hold values from 0.5 to 2
- rho_bar: float32 [32], replicated, may hold values from 0.5 to 2
- phi_bar: float32 [32], replicated, may hold values from 0.5 to 2
Outputs:
- station_out: float32 [2, 32, 4096], P(None, 'src', 'sta')
- source_out: float32 [2, 32, 32768], P(None, 'sta', 'src')
- search_out: float32 [2, 32, 32768], P(None, 'sta', 'src')
- solution_out: float32 [2, 32, 32768], P(None, 'sta', 'src')
- alpha_out: float32 [32], replicated
- rho_bar_out: float32 [32], replicated
- phi_bar_out: float32 [32], replicated
All inputs are finite; a program needn't handle non-finite values.
Results may differ from a plain program's by a relative error of at most 0.019.
Values may be sent and summed in bfloat16 or wider, within the bound.
A program may use at most 64 MiB of HBM per device.

v0:
```python
import jax
import jax.numpy as jnp
from jax import lax
from jax.sharding import PartitionSpec as P

ITERS = 3


epsilon = 1e-06


def sent_to_all(array, axis):
    copies = jnp.broadcast_to(array, (lax.axis_size(axis), *array.shape))
    return lax.all_to_all(copies, axis, split_axis=0, concat_axis=0, tiled=True)


def in_order(pieces, dim):
    shape = list(pieces.shape[1:])
    shape[dim] *= pieces.shape[0]
    return jnp.moveaxis(pieces, 0, dim).reshape(shape)


def gather_directly(array, axis, dim):
    pieces = sent_to_all(array, axis)
    return in_order(pieces, dim)


def taken_together(array, axis):
    return sent_to_all(array, axis).sum(axis=0)


def padded_to(lines, peers):
    spare = -len(lines) % peers
    return jnp.pad(lines, [(0, spare)] + [(0, 0)] * (lines.ndim - 1))


def cut_along(array, dim, peers):
    shape = array.shape
    pieces = array.reshape(*shape[:dim], peers, shape[dim] // peers, *shape[dim + 1 :])
    return jnp.moveaxis(pieces, dim, 0)


def sum_at_owner(array, axis, dim):
    peers = lax.axis_size(axis)
    pieces = lax.all_to_all(cut_along(array, dim, peers), axis, 0, 0, tiled=True)
    return jnp.sum(pieces, axis=0)


def nested_sum(array, axes):
    lines = array.reshape(-1, array.shape[-1])
    padded = padded_to(lines, lax.axis_size(axes))
    whole = gather_directly(sum_at_owner(padded, axes, 0), axes, 0)
    return lax.slice_in_dim(whole, 0, len(lines)).reshape(array.shape)


def forward_apply(green_real, green_imag, pair):
    contract = (((1,), (1,)), ((), ()))
    real_real = lax.dot_general(pair[0], green_real, contract, preferred_element_type=jnp.float32)
    imag_imag = lax.dot_general(pair[1], green_imag, contract, preferred_element_type=jnp.float32)
    real_imag = lax.dot_general(pair[0], green_imag, contract, preferred_element_type=jnp.float32)
    imag_real = lax.dot_general(pair[1], green_real, contract, preferred_element_type=jnp.float32)
    return jnp.stack((real_real - imag_imag, imag_real + real_imag))


def adjoint_apply(green_real, green_imag, pair):
    contract = (((1,), (0,)), ((), ()))
    real_real = lax.dot_general(pair[0], green_real, contract, preferred_element_type=jnp.float32)
    imag_imag = lax.dot_general(pair[1], green_imag, contract, preferred_element_type=jnp.float32)
    imag_real = lax.dot_general(pair[1], green_real, contract, preferred_element_type=jnp.float32)
    real_imag = lax.dot_general(pair[0], green_imag, contract, preferred_element_type=jnp.float32)
    return jnp.stack((real_real + imag_imag, imag_real - real_imag))


def rotate(alpha_now, beta_now, rho_bar, phi_bar):
    rho_new = jnp.sqrt(rho_bar * rho_bar + beta_now * beta_now)
    cosine = rho_bar / rho_new
    sine_val = beta_now / rho_new
    theta_val = sine_val * alpha_now
    phi_val = cosine * phi_bar
    return (-cosine * alpha_now, sine_val * phi_bar, phi_val / rho_new, theta_val / rho_new)


def shards(
    green_real,
    green_imag,
    station_vec,
    source_vec,
    search_dir,
    solution,
    alpha_now,
    rho_bar,
    phi_bar,
):
    rows_total = green_real.shape[0] * lax.axis_size("sta")
    cols_total = green_real.shape[1] * lax.axis_size("src")
    ratio = cols_total / rows_total
    events = alpha_now.shape[0]
    own_src = events // lax.axis_size("src")
    own_sta = events // lax.axis_size("sta")
    src_first = lax.axis_index("src") * own_src
    sta_first = lax.axis_index("sta") * own_sta
    station_all = gather_directly(station_vec, "src", 1)
    source_all = gather_directly(source_vec, "sta", 1)
    for iteration in range(ITERS):
        partial_image = forward_apply(green_real, green_imag, source_all.astype(jnp.bfloat16))
        image = taken_together(partial_image, "src")
        station_all = image - alpha_now[None, :, None] * station_all
        squares = taken_together(jnp.sum(station_all * station_all, axis=(0, 2)), "sta")
        beta_now = jnp.sqrt(squares / rows_total + epsilon)
        station_all = station_all / beta_now[None, :, None]
        partial_back = adjoint_apply(green_real, green_imag, station_all.astype(jnp.bfloat16))
        back = nested_sum(partial_back, "sta")
        source_all = ratio * back - beta_now[None, :, None] * source_all
        col_squares = taken_together(jnp.sum(source_all * source_all, axis=(0, 2)), "src")
        alpha_now = jnp.sqrt(col_squares / cols_total + epsilon)
        source_all = source_all / alpha_now[None, :, None]
        rho_bar, phi_bar, step_sol, step_dir = rotate(alpha_now, beta_now, rho_bar, phi_bar)
        local_source = lax.dynamic_slice_in_dim(source_all, sta_first, own_sta, 1)
        local_sol = lax.dynamic_slice_in_dim(step_sol, sta_first, own_sta, 0)
        local_dir = lax.dynamic_slice_in_dim(step_dir, sta_first, own_sta, 0)
        solution = solution + local_sol[None, :, None] * search_dir
        search_dir = local_source - local_dir[None, :, None] * search_dir
    station_vec = lax.dynamic_slice_in_dim(station_all, src_first, own_src, 1)
    source_vec = lax.dynamic_slice_in_dim(source_all, sta_first, own_sta, 1)
    return (station_vec, source_vec, search_dir, solution, alpha_now, rho_bar, phi_bar)


def solution(mesh):
    placed = (
        P("sta", "src"),
        P("sta", "src"),
        P(None, "src", "sta"),
        P(None, "sta", "src"),
        P(None, "sta", "src"),
        P(None, "sta", "src"),
        P(),
        P(),
        P(),
    )
    return jax.shard_map(
        shards,
        mesh=mesh,
        in_specs=placed,
        out_specs=(
            P(None, "src", "sta"),
            P(None, "sta", "src"),
            P(None, "sta", "src"),
            P(None, "sta", "src"),
            P(),
            P(),
            P(),
        ),
        check_vma=False,
    )
```

profile of v0, /device:TPU:1, one launch (start us, length us, event | category | flops | bytes accessed | tf_op | source)
XLA Modules:
  0.0 535.4 jit_solution(9207313944046148172)
XLA Ops:
  0.6 0.8 copy.115
  1.7 42.6 %all_to_all.91 = f32[32,2,1,2048]{3,1,2,0:T(2,128)S(1)} all-to-all(f32[32,2,1,2048]{3,1,2,0:T(2,128)S(1)} %broadcast_in_dim.66), channel_id=1, replica_groups=mesh['sta'=32,'src'=16] {'sta'}, dimensions={0} | all-to-all | bytes 1048576 | tf_op jit(solution)/shard_map/all_to_all | solution.py:14
  45.2 0.5 copy-done.1
  46.3 39.2 %all_to_all.92 = f32[16,2,32,128]{3,2,1,0:T(8,128)S(1)} all-to-all(f32[16,2,32,128]{3,2,1,0:T(8,128)S(1)} %broadcast_in_dim.67), channel_id=1, replica_groups=mesh['sta'=32,'src'=16] {'src'}, dimensions={0} | all-to-all | bytes 1048576 | tf_op jit(solution)/shard_map/all_to_all | solution.py:14
  85.5 0.6 broadcast_in_dim.68
  86.1 4.4 all-to-all-start.2
  90.6 14.5 %all-to-all-done.2 = f32[16,2,2,128]{3,2,1,0:T(2,128)S(1)} async-done(((f32[16,2,2,128]{3,2,1,0:T(2,128)}), f32[16,2,2,128]{3,2,1,0:T(2,128)S(1)}, u32[]{:S(2)}, u32[]{:S(2)}) %all-to-all-start.2) | async-done | bytes 32800 | tf_op jit(solution)/shard_map/all_to_all | solution.py:14
  105.3 0.6 broadcast_in_dim.70
  105.9 14.3 %all-to-all-start.3 = ((f32[32,1,32]{2,1,0:T(1,128)}), f32[32,1,32]{2,1,0:T(1,128)S(1)}, u32[]{:S(2)}, u32[]{:S(2)}) async-start(f32[32,1,32]{2,1,0:T(1,128)} %broadcast_in_dim.70), calls=%async_computation.3 | async-start | bytes 32768 | tf_op jit(solution)/shard_map/all_to_all | solution.py:14
  120.3 11.4 %all-to-all-done.3 = f32[32,1,32]{2,1,0:T(1,128)S(1)} async-done(((f32[32,1,32]{2,1,0:T(1,128)}), f32[32,1,32]{2,1,0:T(1,128)S(1)}, u32[]{:S(2)}, u32[]{:S(2)}) %all-to-all-start.3) | async-done | bytes 4128 | tf_op jit(solution)/shard_map/all_to_all | solution.py:14
  132.9 29.7 %all_to_all.93 = f32[32,2,2048]{2,1,0:T(2,128)S(1)} all-to-all(f32[32,2,2048]{2,1,0:T(2,128)S(1)} %reshape.224), channel_id=1, replica_groups=mesh['sta'=32,'src'=16] {'sta'}, dimensions={0} | all-to-all | bytes 1048576 | tf_op jit(solution)/shard_map/all_to_all | solution.py:45
  162.8 1.0 broadcast_in_dim.71
  163.8 8.6 %all-to-all-start.5 = ((f32[32,2,2048]{2,1,0:T(2,128)}), f32[32,2,2048]{2,1,0:T(2,128)S(1)}, u32[]{:S(2)}, u32[]{:S(2)}) async-start(f32[32,2,2048]{2,1,0:T(2,128)} %broadcast_in_dim.71), calls=%async_computation.5 | async-start | bytes 1048576 | tf_op jit(solution)/shard_map/all_to_all | solution.py:14
  172.4 0.3 copy.114
  172.7 0.3 reshape.225
  173.1 26.0 %all-to-all-done.5 = f32[32,2,2048]{2,1,0:T(2,128)S(1)} async-done(((f32[32,2,2048]{2,1,0:T(2,128)}), f32[32,2,2048]{2,1,0:T(2,128)S(1)}, u32[]{:S(2)}, u32[]{:S(2)}) %all-to-all-start.5) | async-done | bytes 524320 | tf_op jit(solution)/shard_map/all_to_all | solution.py:14
  199.2 0.5 broadcast_multiply_fusion.2
  199.8 0.6 broadcast_in_dim.72
  200.4 7.1 %all-to-all-start.6 = ((f32[16,1,32]{2,1,0:T(1,128)}), f32[16,1,32]{2,1,0:T(1,128)S(1)}, u32[]{:S(2)}, u32[]{:S(2)}) async-start(f32[16,1,32]{2,1,0:T(1,128)} %broadcast_in_dim.72), calls=%async_computation.6 | async-start | bytes 16384 | tf_op jit(solution)/shard_map/all_to_all | solution.py:14
  207.5 1.1 mul.270
  208.7 13.1 %all-to-all-done.6 = f32[16,1,32]{2,1,0:T(1,128)S(1)} async-done(((f32[16,1,32]{2,1,0:T(1,128)}), f32[16,1,32]{2,1,0:T(1,128)S(1)}, u32[]{:S(2)}, u32[]{:S(2)}) %all-to-all-start.6) | async-done | bytes 2080 | tf_op jit(solution)/shard_map/all_to_all | solution.py:14
  221.8 1.4 fusion.43
  224.3 0.9 broadcast_in_dim.73
  225.2 4.0 all-to-all-start.7
  229.3 25.5 %all-to-all-done.7 = f32[16,2,32,128]{3,2,1,0:T(8,128)S(1)} async-done(((f32[16,2,32,128]{3,2,1,0:T(8,128)}), f32[16,2,32,128]{3,2,1,0:T(8,128)S(1)}, u32[]{:S(2)}, u32[]{:S(2)}) %all-to-all-start.7) | async-done | bytes 524320 | tf_op jit(solution)/shard_map/all_to_all | solution.py:14
  255.1 25.3 %all_to_all.94 = f32[32,1,32]{2,1,0:T(1,128)S(1)} all-to-all(f32[32,1,32]{2,1,0:T(1,128)S(1)} %broadcast_in_dim.75), channel_id=1, replica_groups=mesh['sta'=32,'src'=16] {'sta'}, dimensions={0} | all-to-all | bytes 8192 | tf_op jit(solution)/shard_map/all_to_all | solution.py:14
  281.4 1.1 reshape.226
  282.5 29.4 %all_to_all.95 = f32[32,2,2048]{2,1,0:T(2,128)S(1)} all-to-all(f32[32,2,2048]{2,1,0:T(2,128)} %reshape.226), channel_id=1, replica_groups=mesh['sta'=32,'src'=16] {'sta'}, dimensions={0} | all-to-all | bytes 1048576 | tf_op jit(solution)/shard_map/all_to_all | solution.py:45
  312.1 1.0 broadcast_in_dim.76
  313.1 9.7 %all-to-all-start.10 = ((f32[32,2,2048]{2,1,0:T(2,128)}), f32[32,2,2048]{2,1,0:T(2,128)S(1)}, u32[]{:S(2)}, u32[]{:S(2)}) async-start(f32[32,2,2048]{2,1,0:T(2,128)} %broadcast_in_dim.76), calls=%async_computation.10 | async-start | bytes 1048576 | tf_op jit(solution)/shard_map/all_to_all | solution.py:14
  323.0 26.7 %all-to-all-done.10 = f32[32,2,2048]{2,1,0:T(2,128)S(1)} async-done(((f32[32,2,2048]{2,1,0:T(2,128)}), f32[32,2,2048]{2,1,0:T(2,128)S(1)}, u32[]{:S(2)}, u32[]{:S(2)}) %all-to-all-start.10) | async-done | bytes 524320 | tf_op jit(solution)/shard_map/all_to_all | solution.py:14
  349.6 0.8 copy-done.2
  350.4 2.6 multiply_reduce_fusion.1
  353.1 0.6 broadcast_in_dim.77
  353.8 7.3 %all-to-all-start.11 = ((f32[16,1,32]{2,1,0:T(1,128)}), f32[16,1,32]{2,1,0:T(1,128)S(1)}, u32[]{:S(2)}, u32[]{:S(2)}) async-start(f32[16,1,32]{2,1,0:T(1,128)} %broadcast_in_dim.77), calls=%async_computation.11 | async-start | bytes 16384 | tf_op jit(solution)/shard_map/all_to_all | solution.py:14
  361.0 1.4 mul.284
  362.4 12.7 %all-to-all-done.11 = f32[16,1,32]{2,1,0:T(1,128)S(1)} async-done(((f32[16,1,32]{2,1,0:T(1,128)}), f32[16,1,32]{2,1,0:T(1,128)S(1)}, u32[]{:S(2)}, u32[]{:S(2)}) %all-to-all-start.11) | async-done | bytes 2080 | tf_op jit(solution)/shard_map/all_to_all | solution.py:14
  376.5 0.9 broadcast_in_dim.78
  377.4 4.0 all-to-all-start.12
  381.5 25.5 %all-to-all-done.12 = f32[16,2,32,128]{3,2,1,0:T(8,128)S(1)} async-done(((f32[16,2,32,128]{3,2,1,0:T(8,128)}), f32[16,2,32,128]{3,2,1,0:T(8,128)S(1)}, u32[]{:S(2)}, u32[]{:S(2)}) %all-to-all-start.12) | async-done | bytes 524320 | tf_op jit(solution)/shard_map/all_to_all | solution.py:14
  407.3 25.3 %all_to_all.96 = f32[32,1,32]{2,1,0:T(1,128)S(1)} all-to-all(f32[32,1,32]{2,1,0:T(1,128)S(1)} %broadcast_in_dim.80), channel_id=1, replica_groups=mesh['sta'=32,'src'=16] {'sta'}, dimensions={0} | all-to-all | bytes 8192 | tf_op jit(solution)/shard_map/all_to_all | solution.py:14
  432.6 0.6 copy-done.7
  433.2 0.6 multiply_multiply_fusion
  435.1 28.6 %all_to_all.97 = f32[32,2,2048]{2,1,0:T(2,128)S(1)} all-to-all(f32[32,2,2048]{2,1,0:T(2,128)S(1)} %reshape.227), channel_id=1, replica_groups=mesh['sta'=32,'src'=16] {'sta'}, dimensions={0} | all-to-all | bytes 1048576 | tf_op jit(solution)/shard_map/all_to_all | solution.py:45
  463.8 1.0 broadcast_in_dim.81
  464.9 9.7 %all-to-all-start.15 = ((f32[32,2,2048]{2,1,0:T(2,128)}), f32[32,2,2048]{2,1,0:T(2,128)S(1)}, u32[]{:S(2)}, u32[]{:S(2)}) async-start(f32[32,2,2048]{2,1,0:T(2,128)} %broadcast_in_dim.81), calls=%async_computation.15 | async-start | bytes 1048576 | tf_op jit(solution)/shard_map/all_to_all | solution.py:14
  474.7 26.7 %all-to-all-done.15 = f32[32,2,2048]{2,1,0:T(2,128)S(1)} async-done(((f32[32,2,2048]{2,1,0:T(2,128)}), f32[32,2,2048]{2,1,0:T(2,128)S(1)}, u32[]{:S(2)}, u32[]{:S(2)}) %all-to-all-start.15) | async-done | bytes 524320 | tf_op jit(solution)/shard_map/all_to_all | solution.py:14
  501.3 0.6 broadcast_multiply_fusion
  502.1 0.6 broadcast_in_dim.82
  502.7 7.3 %all-to-all-start.16 = ((f32[16,1,32]{2,1,0:T(1,128)}), f32[16,1,32]{2,1,0:T(1,128)S(1)}, u32[]{:S(2)}, u32[]{:S(2)}) async-start(f32[16,1,32]{2,1,0:T(1,128)} %broadcast_in_dim.82), calls=%async_computation.16 | async-start | bytes 16384 | tf_op jit(solution)/shard_map/all_to_all | solution.py:14
  510.0 0.6 constant_dynamic-slice_fusion
  510.6 0.6 dynamic-slice
  511.1 0.4 mul.299
  511.5 12.6 %all-to-all-done.16 = f32[16,1,32]{2,1,0:T(1,128)S(1)} async-done(((f32[16,1,32]{2,1,0:T(1,128)}), f32[16,1,32]{2,1,0:T(1,128)S(1)}, u32[]{:S(2)}, u32[]{:S(2)}) %all-to-all-start.16) | async-done | bytes 2080 | tf_op jit(solution)/shard_map/all_to_all | solution.py:14
  524.1 0.5 negate_multiply_fusion
  524.7 0.7 dynamic-slice.1
  525.4 0.6 dynamic_slice.35
  526.0 0.6 dynamic_slice.37
  526.6 0.6 dynamic_slice.38
  527.2 0.6 dynamic_slice.39
  527.8 0.6 dynamic_slice.40
  528.4 0.6 dynamic_slice.33
  529.0 3.8 multiply_add_fusion
  532.9 2.5 multiply_subtract_fusion.3
  (99 shorter events, 10.1 us)
Async XLA Ops:
  0.6 44.0 %copy-start = (bf16[128,2048]{1,0:T(8,128)(2,1)S(1)}, bf16[128,2048]{1,0:T(8,128)(2,1)}, u32[]{:S(2)}) copy-start(bf16[128,2048]{1,0:T(8,128)(2,1)} %param.9) | copy-start | bytes 1572868
  44.6 1.0 copy-start.1
  46.3 39.2 %copy-start.6 = (f32[2,2,128]{2,1,0:T(2,128)S(1)}, f32[2,2,128]{2,1,0:T(2,128)}, u32[]{:S(2)}) copy-start(f32[2,2,128]{2,1,0:T(2,128)} %param.11) | copy-start | bytes 6148
  86.1 4.4 copy-start.5
  86.1 19.0 %all-to-all-start.2 = ((f32[16,2,2,128]{3,2,1,0:T(2,128)}), f32[16,2,2,128]{3,2,1,0:T(2,128)S(1)}, u32[]{:S(2)}, u32[]{:S(2)}) async-start(f32[16,2,2,128]{3,2,1,0:T(2,128)} %broadcast_in_dim.68), calls=%async_computation.2 | async-start | bytes 65536 | tf_op jit(solution)/shard_map/all_to_all | solution.py:14
  105.9 25.7 %all-to-all-start.3 = ((f32[32,1,32]{2,1,0:T(1,128)}), f32[32,1,32]{2,1,0:T(1,128)S(1)}, u32[]{:S(2)}, u32[]{:S(2)}) async-start(f32[32,1,32]{2,1,0:T(1,128)} %broadcast_in_dim.70), calls=%async_computation.3 | async-start | bytes 32768 | tf_op jit(solution)/shard_map/all_to_all | solution.py:14
  163.8 35.4 %all-to-all-start.5 = ((f32[32,2,2048]{2,1,0:T(2,128)}), f32[32,2,2048]{2,1,0:T(2,128)S(1)}, u32[]{:S(2)}, u32[]{:S(2)}) async-start(f32[32,2,2048]{2,1,0:T(2,128)} %broadcast_in_dim.71), calls=%async_computation.5 | async-start | bytes 1048576 | tf_op jit(solution)/shard_map/all_to_all | solution.py:14
  200.4 21.3 %all-to-all-start.6 = ((f32[16,1,32]{2,1,0:T(1,128)}), f32[16,1,32]{2,1,0:T(1,128)S(1)}, u32[]{:S(2)}, u32[]{:S(2)}) async-start(f32[16,1,32]{2,1,0:T(1,128)} %broadcast_in_dim.72), calls=%async_computation.6 | async-start | bytes 16384 | tf_op jit(solution)/shard_map/all_to_all | solution.py:14
  225.2 29.6 %all-to-all-start.7 = ((f32[16,2,32,128]{3,2,1,0:T(8,128)}), f32[16,2,32,128]{3,2,1,0:T(8,128)S(1)}, u32[]{:S(2)}, u32[]{:S(2)}) async-start(f32[16,2,32,128]{3,2,1,0:T(8,128)} %broadcast_in_dim.73), calls=%async_computation.7 | async-start | bytes 1048576 | tf_op jit(solution)/shard_map/all_to_all | solution.py:14
  313.1 36.5 %all-to-all-start.10 = ((f32[32,2,2048]{2,1,0:T(2,128)}), f32[32,2,2048]{2,1,0:T(2,128)S(1)}, u32[]{:S(2)}, u32[]{:S(2)}) async-start(f32[32,2,2048]{2,1,0:T(2,128)} %broadcast_in_dim.76), calls=%async_computation.10 | async-start | bytes 1048576 | tf_op jit(solution)/shard_map/all_to_all | solution.py:14
  349.6 0.8 copy-start.2
  353.8 21.4 %all-to-all-start.11 = ((f32[16,1,32]{2,1,0:T(1,128)}), f32[16,1,32]{2,1,0:T(1,128)S(1)}, u32[]{:S(2)}, u32[]{:S(2)}) async-start(f32[16,1,32]{2,1,0:T(1,128)} %broadcast_in_dim.77), calls=%async_computation.11 | async-start | bytes 16384 | tf_op jit(solution)/shard_map/all_to_all | solution.py:14
  377.4 29.6 %all-to-all-start.12 = ((f32[16,2,32,128]{3,2,1,0:T(8,128)}), f32[16,2,32,128]{3,2,1,0:T(8,128)S(1)}, u32[]{:S(2)}, u32[]{:S(2)}) async-start(f32[16,2,32,128]{3,2,1,0:T(8,128)} %broadcast_in_dim.78), calls=%async_computation.12 | async-start | bytes 1048576 | tf_op jit(solution)/shard_map/all_to_all | solution.py:14
  432.6 0.7 copy-start.7
  432.6 0.7 copy-start.9
  464.9 36.5 %all-to-all-start.15 = ((f32[32,2,2048]{2,1,0:T(2,128)}), f32[32,2,2048]{2,1,0:T(2,128)S(1)}, u32[]{:S(2)}, u32[]{:S(2)}) async-start(f32[32,2,2048]{2,1,0:T(2,128)} %broadcast_in_dim.81), calls=%async_computation.15 | async-start | bytes 1048576 | tf_op jit(solution)/shard_map/all_to_all | solution.py:14
  502.7 21.4 %all-to-all-start.16 = ((f32[16,1,32]{2,1,0:T(1,128)}), f32[16,1,32]{2,1,0:T(1,128)S(1)}, u32[]{:S(2)}, u32[]{:S(2)}) async-start(f32[16,1,32]{2,1,0:T(1,128)} %broadcast_in_dim.82), calls=%async_computation.16 | async-start | bytes 16384 | tf_op jit(solution)/shard_map/all_to_all | solution.py:14
  524.7 0.7 copy-start.8
  525.4 3.7 copy-start.3
  525.4 3.6 copy-start.4
where the time goes:
time: 537 us; the launch traced here: 535 us
  blocking collectives  220 us (41%)
  waiting for transfers between devices  195 us (36%)
  starting transfers between devices  76.4 us (14%)
  local copies, waits for them, and re-layouts  22.9 us (4%)
  other arithmetic  14.6 us (3%)
  matrix products  5.87 us (1%)
    all_to_all x10, waiting for transfers between devices, sent_to_all(): return lax.all_to_all(copies, axis, split_axis=0, concat_axis=0, tiled=True)  195 us
    all_to_all x4, blocking collectives, sent_to_all(): return lax.all_to_all(copies, axis, split_axis=0, concat_axis=0, tiled=True)  132 us
    all_to_all x3, blocking collectives, sum_at_owner(): lax.all_to_all(cut_along(array, dim, peers), axis, 0, 0, tiled=True)  87.7 us
    all_to_all x10, starting transfers between devices, sent_to_all(): return lax.all_to_all(copies, axis, split_axis=0, concat_axis=0, tiled=True)  76.4 us
  transfers between devices with their start and end apart: 10, of which 10 were waited for; matrix products, arithmetic and copies ran while one was open for 1% of the time, Pallas kernels for 0%

commit v1 on v0

v1 whole, which is shorter than its diff:
```python
import functools

import jax
import jax.numpy as jnp
from jax import lax
from jax.experimental import pallas as pl
from jax.experimental.pallas import tpu as pltpu
from jax.sharding import PartitionSpec as P

ITERS = 3
EPS = 1e-06
MESH = pl.DeviceIdType.MESH
F32 = jnp.float32
BF16 = jnp.bfloat16
LANES = 128
PART = 8


class Grid:
    def __init__(self, ny, nq, nhalf, nzh, nx, ncore):
        self.ny, self.nq, self.nhalf = ny, nq, nhalf
        self.nzh, self.nx, self.ncore = nzh, nx, ncore
        self.nz = nq * nhalf
        self.nxc = nx * ncore
        self.groups = 2 * self.nz // PART
        self.per = self.nz // self.groups


FULL = Grid(4, 4, 2, 2, 4, 2)


def kernel(grid, rows_total, cols_total, *refs):
    (green_re, green_im, station_ref, source_ref, search_ref, sol_ref,
     alpha_ref, rho_ref, phi_ref,
     station_out, source_out, search_out, sol_out, alpha_out, rho_out, phi_out,
     gmat, first, first_rows, vall, a1_out, a1_in, a2_in, af_out, af_in, ag_in,
     b1_out, b1_in, b2_out, b2_in, b3_out, b3_in,
     uhat, unorm, coef,
     load_sem, first_send, first_recv, send, recv) = refs
    ny, nq, nxc, groups, per = grid.ny, grid.nq, grid.nxc, grid.groups, grid.per
    width = source_ref.shape[-1] // nq
    half_rows = ny // 2
    ratio = cols_total / rows_total

    sta = lax.axis_index("sta")
    src = lax.axis_index("src")
    y = lax.rem(sta, ny)
    z = lax.div(sta, ny)
    quad = lax.rem(z, nq)
    zhalf = lax.div(z, nq)
    zh = lax.div(src, nxc)
    xc = lax.rem(src, nxc)
    core = lax.rem(xc, 2)

    def device(dz=None, dy=None, sta_to=None, src_to=None):
        return {"sta": sta if sta_to is None else sta_to, "src": src if src_to is None else src_to}

    def y_peer(d):
        return lax.rem(y + d, ny)

    def sta_of(z_at, y_at):
        return z_at * ny + y_at

    y_order = sorted(range(1, ny), key=lambda d: -min(d, ny - d))
    peers = []
    for d in range(1, ny):
        peers.append(device(sta_to=sta_of(z, y_peer(d))))
    for d in range(1, grid.nz):
        peers.append(device(sta_to=sta_of(lax.rem(z + d, grid.nz), y)))
    for d in range(1, nxc):
        peers.append(device(src_to=zh * nxc + lax.rem(xc + d, nxc)))
    other = (1 - zh) * nxc + xc - core
    for c in range(2):
        peers.append(device(src_to=other + c))
    barrier = pltpu.get_barrier_semaphore()
    for peer in peers:
        pl.semaphore_signal(barrier, inc=1, device_id=peer, device_id_type=MESH)

    rows_half = green_re.shape[0]
    loads = [
        pltpu.make_async_copy(green_re, gmat.at[pl.ds(0, rows_half)], load_sem.at[0]),
        pltpu.make_async_copy(green_im, gmat.at[pl.ds(rows_half, rows_half)], load_sem.at[1]),
    ]
    for load in loads:
        load.start()

    own = source_ref[:, 0, :]
    pieces = [own[p : p + 1, q * width : (q + 1) * width] for p in range(2) for q in range(nq)]
    first[z] = jnp.concatenate(pieces, axis=0).astype(BF16)

    sends = []

    def remote(src_at, dst_at, send_sem, recv_sem, to):
        copy = pltpu.make_async_remote_copy(
            src_ref=src_at, dst_ref=dst_at, send_sem=send_sem, recv_sem=recv_sem,
            device_id=to, device_id_type=MESH)
        copy.start()

    def wait_bytes(ref, sem):
        pltpu.make_async_copy(ref, ref, sem).wait()

    def is_re(shape):
        return lax.broadcasted_iota(jnp.int32, shape, len(shape) - 2) < per

    def swap(a):
        return pltpu.roll(a, per, a.ndim - 2)

    def encode(total):
        high = total.astype(BF16).astype(F32)
        return jnp.where(is_re(total.shape), high, total - high)

    def decode(pair):
        return pair + swap(pair)

    def lanes(a):
        return jnp.broadcast_to(a, a.shape[:-1] + (LANES,))

    def event_of(k, shape):
        zl = lax.rem(lax.broadcasted_iota(jnp.int32, shape, 1), per)
        return (k * per + zl) * ny + lax.broadcasted_iota(jnp.int32, shape, 0)

    n_events = alpha_ref.shape[-1]

    def spread(ref, k):
        shape = (ny, PART, n_events)
        lane = lax.broadcasted_iota(jnp.int32, shape, 2)
        row = jnp.broadcast_to(ref[...].reshape(1, 1, n_events), shape)
        return lanes(jnp.sum(jnp.where(lane == event_of(k, shape), row, 0.0), axis=-1, keepdims=True))

    alpha = [spread(alpha_ref, k) for k in range(groups)]
    rho = [spread(rho_ref, k) for k in range(groups)]
    phi = [spread(phi_ref, k) for k in range(groups)]

    search_out[...] = search_ref[...]
    sol_out[...] = sol_ref[...]

    for load in loads:
        load.wait()
    pl.semaphore_wait(barrier, len(peers))

    for d in range(1, grid.nz):
        remote(first.at[z], first.at[z], first_send, first_recv,
               device(sta_to=sta_of(lax.rem(z + d, grid.nz), y)))
    wait_bytes(first.at[pl.ds(0, grid.nz - 1)], first_recv)
    for k in range(groups):
        for e in range(per):
            block = first[k * per + e].astype(F32)
            for p in range(2):
                for q in range(nq):
                    first_rows[k, q, p * per + e : p * per + e + 1, :] = block[p * nq + q : p * nq + q + 1, :]
        vall[0, k, y, :, :, 0:width] = first_rows[k].astype(BF16)

    def share_y(t, k):
        for d in y_order:
            remote(vall.at[t, k, y], vall.at[t, k, y], send.at[t, k, 6], recv.at[t, k, 6],
                   device(sta_to=sta_of(z, y_peer(d))))

    for k in range(groups):
        share_y(0, k)

    def columns(t, k, q):
        return vall[t, k, :, q, :, 0:width].astype(F32)

    def beta_squares(t, k):
        return decode(vall[t, k, :, 0, :, width:].astype(F32))

    def root(total, count):
        return jnp.sqrt(total * (1.0 / count) + EPS)

    def squares_of(values):
        total = jnp.sum(values[0] * values[0], axis=-1, keepdims=True)
        for value in values[1:]:
            total += jnp.sum(value * value, axis=-1, keepdims=True)
        return lanes(total + swap(lanes(total))[..., 0:1])

    contract = (((1,), (1,)), ((), ()))

    def stage_a1(t, k):
        wait_bytes(vall.at[t, k, pl.ds(0, ny - 1)], recv.at[t, k, 6])
        values = [columns(t, k, q) for q in range(nq)]
        last = t == ITERS
        buf_out, buf_in = (af_out.at[k], af_in.at[k]) if last else (a1_out.at[t, k], a1_in.at[t, k])
        if t == 0:
            scalars = jnp.zeros((ny, PART, LANES), F32)
        else:
            scalars = encode(squares_of(values))
        if last:
            message = scalars
        else:
            product = jnp.zeros((ny * PART, 2 * rows_half), F32)
            for q in range(nq):
                left = values[q].reshape(ny * PART, width).astype(BF16)
                product += lax.dot_general(
                    left, gmat[:, q * width : (q + 1) * width], contract, preferred_element_type=F32)
            product = product.reshape(ny, PART, 2 * rows_half)
            turned = swap(product[..., rows_half:])
            image = product[..., :rows_half] + jnp.where(is_re(turned.shape), -turned, turned)
            if t == 0:
                shape = image.shape
                event = event_of(k, shape)
                part_re = is_re(shape)
                per_src = station_ref.shape[1]
                for n in range(per_src):
                    mine = event == src * per_src + n
                    both = jnp.where(part_re, jnp.broadcast_to(station_ref[0, n : n + 1, :][None], shape),
                                     jnp.broadcast_to(station_ref[1, n : n + 1, :][None], shape))
                    image -= jnp.where(mine, alpha[k] * both, 0.0)
            message = jnp.concatenate([image, scalars], axis=-1)
        message = message.astype(BF16)
        for c in range(2):
            buf_out[c] = message[c * half_rows : (c + 1) * half_rows]
        buf_in[xc] = buf_out[core]
        for d in range(1, nxc):
            to = lax.rem(xc + d, nxc)
            remote(buf_out.at[lax.rem(to, 2)], buf_in.at[xc], send.at[t, k, 0], recv.at[t, k, 0],
                   device(src_to=zh * nxc + to))

    def stage_a2(t, k):
        last = t == ITERS
        buf_in, buf_next = (af_in.at[k], ag_in.at[k]) if last else (a1_in.at[t, k], a2_in.at[t, k])
        wait_bytes(buf_in.at[pl.ds(0, nxc - 1)], recv.at[t, k, 0])
        total = buf_in[0].astype(F32)
        for i in range(1, nxc):
            total += buf_in[i].astype(F32)
        scalars = encode(decode(total[..., -LANES:]))
        message = scalars if last else jnp.concatenate([total[..., :rows_half], scalars], axis=-1)
        buf_next[zh * 2 + core] = message.astype(BF16)
        here = buf_next.at[zh * 2 + core]
        for to in (other + core, other + 1 - core, src + 1 - 2 * core):
            remote(here, here, send.at[t, k, 1], recv.at[t, k, 1], device(src_to=to))

    def summed(t, k):
        last = t == ITERS
        buf = ag_in.at[k] if last else a2_in.at[t, k]
        wait_bytes(buf.at[pl.ds(0, 3)], recv.at[t, k, 1])
        halves = [buf[c].astype(F32) + buf[2 + c].astype(F32) for c in range(2)]
        return jnp.concatenate(halves, axis=0)

    def stage_a3(t, k):
        total = summed(t, k)
        vector = total[..., :rows_half]
        if t > 0:
            alpha[k] = root(decode(total[..., -LANES:]), cols_total)
            beta = root(beta_squares(t, k), rows_total)
            vector = vector / alpha[k] - alpha[k] * (uhat[k] / beta)
        uhat[k] = vector
        scalars = encode(squares_of([vector])).astype(BF16)
        turned = swap(vector)
        left = jnp.concatenate([vector, jnp.where(is_re(turned.shape), turned, -turned)], axis=-1)
        left = left.reshape(ny * PART, 2 * rows_half).astype(BF16)
        for q in range(nq):
            back = jnp.dot(left, gmat[:, q * width : (q + 1) * width], preferred_element_type=F32)
            b1_out[t, k, :, q, :, 0:width] = back.reshape(ny, PART, width).astype(BF16)
            b1_out[t, k, :, q, :, width:] = scalars
        for d in y_order:
            remote(b1_out.at[t, k, y_peer(d)], b1_in.at[t, k, y], send.at[t, k, 2], recv.at[t, k, 2],
                   device(sta_to=sta_of(z, y_peer(d))))

    def stage_b2(t, k):
        wait_bytes(b1_in.at[t, k, pl.ds(0, ny - 1)], recv.at[t, k, 2])
        total = b1_out[t, k, y].astype(F32)
        for d in range(1, ny):
            total += b1_in[t, k, y_peer(d)].astype(F32)
        b2_out[t, k, :, :, 0:width] = total[..., :width].astype(BF16)
        b2_out[t, k, :, :, width:] = encode(decode(total[..., width:])).astype(BF16)
        for d in range(1, nq):
            to = lax.rem(quad + d, nq)
            remote(b2_out.at[t, k, to], b2_in.at[t, k, quad], send.at[t, k, 3], recv.at[t, k, 3],
                   device(sta_to=sta_of(zhalf * nq + to, y)))

    def stage_b3(t, k):
        wait_bytes(b2_in.at[t, k, pl.ds(0, nq - 1)], recv.at[t, k, 3])
        total = b2_out[t, k, quad].astype(F32)
        for d in range(1, nq):
            total += b2_in[t, k, lax.rem(quad + d, nq)].astype(F32)
        b3_out[t, k, :, 0:width] = total[:, :width].astype(BF16)
        b3_out[t, k, :, width:] = encode(decode(total[:, width:])).astype(BF16)
        remote(b3_out.at[t, k], b3_in.at[t, k], send.at[t, k, 4], recv.at[t, k, 4],
               device(sta_to=sta_of((1 - zhalf) * nq + quad, y)))

    def stage_b4(t, k):
        wait_bytes(b3_in.at[t, k], recv.at[t, k, 4])
        total = b3_out[t, k].astype(F32) + b3_in[t, k].astype(F32)
        squares = decode(total[:, width:])
        beta = root(squares, rows_total)[:, 0:1]
        before = vall[t, k, y, quad, :, 0:width].astype(F32)
        if t > 0:
            before = before / coef[k, 0, y][:, 0:1]
        after = total[:, :width] * (ratio / beta) - beta * before
        vall[t + 1, k, y, quad, :, 0:width] = after.astype(BF16)
        vall[t + 1, k, y, quad, :, width:] = encode(squares).astype(BF16)
        here = vall.at[t + 1, k, y, quad]
        for d in range(1, nq):
            to = lax.rem(quad + d, nq)
            remote(here, here, send.at[t, k, 5], recv.at[t, k, 5],
                   device(sta_to=sta_of(zhalf * nq + to, y)))

    def stage_b5(t, k):
        wait_bytes(vall.at[t + 1, k, y, pl.ds(0, nq - 1)], recv.at[t, k, 5])
        share_y(t + 1, k)

    mine_k = lax.div(z, per)
    mine_row = lax.rem(z, per)

    def rotate(t, k):
        beta = root(beta_squares(t, k), rows_total)
        rho_new = jnp.sqrt(rho[k] * rho[k] + beta * beta)
        cosine = rho[k] / rho_new
        sine = beta / rho_new
        coef[k, 0] = alpha[k]
        coef[k, 1] = cosine * phi[k] / rho_new
        coef[k, 2] = sine * alpha[k] / rho_new
        rho[k] = -cosine * alpha[k]
        phi[k] = sine * phi[k]

    def step(t):
        def scalar(i):
            return coef[mine_k, i, y, pl.ds(mine_row, 1), :][:, 0:1]

        alpha_own, step_sol, step_dir = scalar(0), scalar(1), scalar(2)
        block = vall[t, mine_k, y].astype(F32)[:, :, 0:width]
        row = lax.broadcasted_iota(jnp.int32, block.shape, 1)
        for p in range(2):
            picked = jnp.sum(jnp.where(row == p * per + mine_row, block, 0.0), axis=1, keepdims=True)
            vector = jnp.concatenate([picked[q] for q in range(nq)], axis=-1) / alpha_own
            before = search_out[p]
            sol_out[p] = sol_out[p] + step_sol * before
            search_out[p] = vector - step_dir * before
            if t == ITERS:
                source_out[p] = vector

    for t in range(ITERS):
        for k in range(groups):
            stage_a1(t, k)
        for k in range(groups):
            stage_a2(t, k)
        for k in range(groups):
            stage_a3(t, k)
        if t > 0:
            for k in range(groups):
                rotate(t, k)
            step(t)
        for stage in (stage_b2, stage_b3, stage_b4, stage_b5):
            for k in range(groups):
                stage(t, k)
    for k in range(groups):
        stage_a1(ITERS, k)
    for k in range(groups):
        unorm[k] = uhat[k] / root(beta_squares(ITERS, k), rows_total)
    per_src = station_ref.shape[1]
    for n in range(per_src):
        event = src * per_src + n
        at_y, at_z = lax.rem(event, ny), lax.div(event, ny)
        for p in range(2):
            station_out[p, n : n + 1, :] = unorm[
                lax.div(at_z, per), at_y, pl.ds(p * per + lax.rem(at_z, per), 1), :]
    for k in range(groups):
        stage_a2(ITERS, k)
    for k in range(groups):
        alpha[k] = root(decode(summed(ITERS, k)), cols_total)
        rotate(ITERS, k)
    step(ITERS)

    def collect(values):
        shape = (ny, PART, n_events)
        lane = lax.broadcasted_iota(jnp.int32, shape, 2)
        total = jnp.zeros((1, n_events), F32)
        for k in range(groups):
            keep = (lane == event_of(k, shape)) & is_re(shape)
            kept = jnp.where(keep, values[k][..., 0:1], 0.0).reshape(ny * PART, n_events)
            total += jnp.sum(kept, axis=0, keepdims=True)
        return total

    alpha_out[...] = collect(alpha)
    rho_out[...] = collect(rho)
    phi_out[...] = collect(phi)

    wait_bytes(first.at[pl.ds(0, grid.nz - 1)], first_send)
    for k in range(groups):
        for t in range(ITERS + 1):
            last = t == ITERS
            wait_bytes((af_in.at[k] if last else a1_in.at[t, k]).at[pl.ds(0, nxc - 1)], send.at[t, k, 0])
            buf = ag_in.at[k] if last else a2_in.at[t, k]
            wait_bytes(buf.at[pl.ds(0, 3)], send.at[t, k, 1])
            wait_bytes(vall.at[t, k, pl.ds(0, ny - 1)], send.at[t, k, 6])
            if not last:
                wait_bytes(b1_in.at[t, k, pl.ds(0, ny - 1)], send.at[t, k, 2])
                wait_bytes(b2_in.at[t, k, pl.ds(0, nq - 1)], send.at[t, k, 3])
                wait_bytes(b3_in.at[t, k], send.at[t, k, 4])
                wait_bytes(vall.at[t, k, 0, pl.ds(0, nq - 1)], send.at[t, k, 5])


def shards(grid, *args):
    green_real, source = args[0], args[3]
    rows = green_real.shape[0]
    rows_total = rows * lax.axis_size("sta")
    cols_total = green_real.shape[1] * lax.axis_size("src")
    ny, nq, groups = grid.ny, grid.nq, grid.groups
    width = green_real.shape[1] // nq
    padded = width + LANES
    n_events = args[6].shape[0]
    args = list(args[:6]) + [a.reshape(1, n_events) for a in args[6:]]
    vmem = pl.BlockSpec(memory_space=pltpu.VMEM)
    half = ny // 2
    message = rows + LANES

    def buf(*shape, kind=BF16):
        return pltpu.VMEM(shape, kind)

    scratch = [
        buf(2 * rows, green_real.shape[1]),
        buf(grid.nz, 2 * nq, width),
        buf(groups, nq, PART, width, kind=F32),
        buf(ITERS + 1, groups, ny, nq, PART, padded),
        buf(ITERS, groups, 2, half, PART, message),
        buf(ITERS, groups, grid.nxc, half, PART, message),
        buf(ITERS, groups, 4, half, PART, message),
        buf(groups, 2, half, PART, LANES),
        buf(groups, grid.nxc, half, PART, LANES),
        buf(groups, 4, half, PART, LANES),
        buf(ITERS, groups, ny, nq, PART, padded),
        buf(ITERS, groups, ny, nq, PART, padded),
        buf(ITERS, groups, nq, PART, padded),
        buf(ITERS, groups, nq, PART, padded),
        buf(ITERS, groups, PART, padded),
        buf(ITERS, groups, PART, padded),
        buf(groups, ny, PART, rows, kind=F32),
        buf(groups, ny, PART, rows, kind=F32),
        buf(groups, 3, ny, PART, LANES, kind=F32),
        pltpu.SemaphoreType.DMA((2,)),
        pltpu.SemaphoreType.DMA,
        pltpu.SemaphoreType.DMA,
        pltpu.SemaphoreType.DMA((ITERS + 1, groups, 7)),
        pltpu.SemaphoreType.DMA((ITERS + 1, groups, 7)),
    ]
    shapes = [args[2].shape, source.shape, source.shape, source.shape] + [(1, n_events)] * 3
    outs = pl.pallas_call(
        functools.partial(kernel, grid, rows_total, cols_total),
        out_shape=[jax.ShapeDtypeStruct(shape, F32) for shape in shapes],
        in_specs=[pl.BlockSpec(memory_space=pl.ANY)] * 2 + [vmem] * 7,
        out_specs=[vmem] * 7,
        scratch_shapes=scratch,
        compiler_params=pltpu.CompilerParams(
            collective_id=0, has_side_effects=True, vmem_limit_bytes=40 * 1024 * 1024),
        name="lsqr",
    )(*args)
    return tuple(outs[:4]) + tuple(a.reshape(n_events) for a in outs[4:])


def build(mesh, grid):
    placed = (
        P("sta", "src"),
        P("sta", "src"),
        P(None, "src", "sta"),
        P(None, "sta", "src"),
        P(None, "sta", "src"),
        P(None, "sta", "src"),
        P(),
        P(),
        P(),
    )
    return jax.shard_map(
        functools.partial(shards, grid),
        mesh=mesh,
        in_specs=placed,
        out_specs=placed[2:],
        check_vma=False,
    )


def solution(mesh):
    return build(mesh, FULL)
```

time: 537 us -> 150 us (0.28)
  blocking collectives: 220 us -> 0 us
  waiting for transfers between devices: 195 us -> 0 us
  Pallas kernels: 0 us -> 140 us
  starting transfers between devices: 76.4 us -> 0 us
  other arithmetic: 14.6 us -> 0 us
  local copies, waits for them, and re-layouts: 22.9 us -> 8.83 us
  matrix products: 5.87 us -> 0 us
    all_to_all x7 -> x0, blocking collectives: 220 us -> none  [the longest x4 132 us: sent_to_all(): return lax.all_to_all(copies, axis, split_axis=0, concat_axis=0, tiled=True)]
    all_to_all x10 -> x0, waiting for transfers between devices: 195 us -> none  [sent_to_all(): return lax.all_to_all(copies, axis, split_axis=0, concat_axis=0, tiled=True)]
    pallas_call x0 -> x1, Pallas kernels: none -> 140 us  [shards(): pl.pallas_call(functools.partial(kernel, grid, rows_total, cols_total), o...]
    all_to_all x10 -> x0, starting transfers between devices: 76.4 us -> none  [sent_to_all(): return lax.all_to_all(copies, axis, split_axis=0, concat_axis=0, tiled=True)]
    broadcast_in_dim x17 -> x0, local copies, waits for them, and re-layouts: 8.4 us -> none  [sent_to_all(): copies = jnp.broadcast_to(array, (lax.axis_size(axis), *array.shape))]
    unnamed x21 -> x25, local copies, waits for them, and re-layouts: 2.73 us -> 8.83 us
    dot_general x24 -> x0, matrix products: 5.87 us -> none  [the longest x3 0.88 us: forward_apply(): lax.dot_general(pair[0], green_imag, contract, preferred_element_type=jnp...]
    dynamic_slice x9 -> x0, local copies, waits for them, and re-layouts: 5.45 us -> none  [the longest x3 1.82 us: shards(): local_dir = lax.dynamic_slice_in_dim(step_dir, sta_first, own_sta, 0)]
  transfers between devices with their start and end apart: 10 -> 0, of which waited for: 10 -> 0; matrix products, arithmetic and copies ran while one was open for 1% -> 0% of each run, Pallas kernels for 0% -> 0%
where the time goes in v1:
time: 150 us
  Pallas kernels  140 us (93%)
  local copies, waits for them, and re-layouts  8.83 us (6%)
    pallas_call x1, Pallas kernels, shards(): pl.pallas_call(functools.partial(kernel, grid, rows_total, cols_total), o...  140 us
    unnamed x25, local copies, waits for them, and re-layouts  8.83 us

profile of v1, /device:TPU:1, one launch (start us, length us, event | category | flops | bytes accessed | tf_op | source)
XLA Modules:
  0.0 149.9 jit_solution(12738853846093188262)
XLA Ops:
  0.6 0.0 copy-start.5
  0.6 0.0 copy-start.6
  0.7 0.0 copy-start.7
  0.7 0.0 copy-start.8
  0.7 0.6 copy-done.5
  1.3 0.0 copy-done.6
  1.3 0.0 copy-done.7
  1.3 0.0 copy-done.8
  1.3 0.0 copy-start
  1.3 1.0 copy-done
  2.4 0.0 copy-start.1
  2.4 1.0 copy-done.1
  3.4 0.0 copy-start.2
  3.4 0.7 copy-done.2
  4.1 0.0 copy-start.3
  4.1 0.7 copy-done.3
  4.9 0.0 copy-start.4
  4.9 0.7 copy-done.4
  5.6 140.4 %lsqr.1 = (f32[2,2,128]{2,1,0:T(2,128)S(1)}, f32[2,1,2048]{2,1,0:T(1,128)S(1)}, f32[2,1,2048]{2,1,0:T(1,128)S(1)}, f32[2,1,2048]{2,1,0:T(1,128)S(1)}, f32[1,32]{...) custom-call(bf16[128,2048]{1,0:T(8,128)(2,1)S(1)} %copy-done, bf16[128,2048]{1,0:T(8,128)(2,1)S(1)} %copy-done.1, ...), custom_call_target="tpu_custom_call" | custom-call | tf_op jit(solution)/shard_map/lsqr/pallas_call | solution.py:437
  146.0 0.6 copy.23
  146.6 0.6 copy.24
  147.2 0.6 copy.25
  147.8 0.6 copy.26
  148.4 0.5 copy.27
  148.9 0.5 copy.28
  149.4 0.5 copy.29
Async XLA Ops:
  0.6 0.7 copy-start.5
  0.6 0.7 copy-start.6
  0.7 0.7 copy-start.7
  0.7 0.7 copy-start.8
  1.3 1.0 copy-start
  2.4 1.0 copy-start.1
  3.4 0.7 copy-start.2
  4.1 0.7 copy-start.3
  4.9 0.7 copy-start.4

commit v2 on v1

v2 whole, which is shorter than its diff:
```python
import functools

import jax
import jax.numpy as jnp
from jax import lax
from jax.experimental import pallas as pl
from jax.experimental.pallas import tpu as pltpu
from jax.sharding import PartitionSpec as P

ITERS = 3
EPS = 1e-06
MESH = pl.DeviceIdType.MESH
F32 = jnp.float32
BF16 = jnp.bfloat16
LANES = 128
PART = 8


class Grid:
    def __init__(self, ny, nq, nhalf, nzh, nx, ncore):
        self.ny, self.nq, self.nhalf = ny, nq, nhalf
        self.nzh, self.nx, self.ncore = nzh, nx, ncore
        self.nz = nq * nhalf
        self.nxc = nx * ncore
        self.groups = 2 * self.nz // PART
        self.per = self.nz // self.groups


FULL = Grid(4, 4, 2, 2, 4, 2)


def kernel(grid, rows_total, cols_total, *refs):
    (green_re, green_im, station_in, source_in, search_in, sol_in, alpha_in, rho_in, phi_in,
     station_out, source_out, search_out, sol_out, alpha_out, rho_out, phi_out,
     station_ref, source_ref, alpha_ref, rho_ref, phi_ref,
     gmat, first, first_rows, vall, a1_out, a1_in, a2_in, fs1, fs2,
     b1_out, b1_in, b2_out, b2_in, b3_out, b3_in,
     uhat, unorm, coef, load_sem, first_send, first_recv, send, recv) = refs
    ny, nq, nxc, groups, per = grid.ny, grid.nq, grid.nxc, grid.groups, grid.per
    n_src = grid.nzh * nxc
    width = source_ref.shape[-1] // nq
    rows_half = gmat.shape[1] // 2
    half_rows = ny // 2
    ratio = cols_total / rows_total
    S_A1, S_A2, S_B2, S_B3, S_B5, S_B1 = 0, 1, 2, 3, 4, 5
    S_B4 = S_B1 + nq

    sta = lax.axis_index("sta")
    src = lax.axis_index("src")
    y = lax.rem(sta, ny)
    z = lax.div(sta, ny)
    quad = lax.rem(z, nq)
    zhalf = lax.div(z, nq)
    zh = lax.div(src, nxc)
    xc = lax.rem(src, nxc)
    core = lax.rem(xc, 2)

    def at_sta(z_at, y_at):
        return {"sta": z_at * ny + y_at, "src": src}

    def at_src(src_to):
        return {"sta": sta, "src": src_to}

    def y_peer(d):
        return lax.rem(y + d, ny)

    def by_distance(i, far_first):
        sign = -1 if far_first else 1
        table = [sorted(range(nq), key=lambda q: sign * abs(q - p))[i] for p in range(nq)]
        value = jnp.int32(table[0])
        for p in range(1, nq):
            value = jnp.where(quad == p, table[p], value)
        return value

    y_order = sorted(range(1, ny), key=lambda d: -min(d, ny - d))
    peers = []
    for d in range(1, grid.nz):
        peers.append(at_sta(lax.rem(z + d, grid.nz), y))
    for d in range(1, ny):
        for e in range(nq):
            peers.append(at_sta(zhalf * nq + lax.rem(quad + e, nq), y_peer(d)))
    for d in range(1, n_src):
        peers.append(at_src(lax.rem(src + d, n_src)))
    barrier = pltpu.get_barrier_semaphore()
    for peer in peers:
        pl.semaphore_signal(barrier, inc=1, device_id=peer, device_id_type=MESH)

    loads = [
        pltpu.make_async_copy(a, b, load_sem.at[i])
        for i, (a, b) in enumerate((
            (source_in, source_ref), (station_in, station_ref), (alpha_in, alpha_ref), (rho_in, rho_ref),
            (phi_in, phi_ref), (search_in, search_out), (sol_in, sol_out)))
    ]
    g_loads = []
    for q in range(nq):
        cut = pl.ds(q * width, width)
        for p, green in enumerate((green_re, green_im)):
            g_loads.append(pltpu.make_async_copy(
                green.at[:, cut], gmat.at[q, pl.ds(p * rows_half, rows_half)],
                load_sem.at[len(loads) + 2 * q + p]))
    for load in loads + g_loads:
        load.start()
    for load in loads:
        load.wait()

    pieces = [source_ref[p, :, q * width : (q + 1) * width] for p in range(2) for q in range(nq)]
    first[z] = jnp.concatenate(pieces, axis=0).astype(BF16)

    def remote(src_at, dst_at, send_sem, recv_sem, to):
        pltpu.make_async_remote_copy(
            src_ref=src_at, dst_ref=dst_at, send_sem=send_sem, recv_sem=recv_sem,
            device_id=to, device_id_type=MESH).start()

    def wait_bytes(ref, sem):
        pltpu.make_async_copy(ref, ref, sem).wait()

    def is_re(shape):
        return lax.broadcasted_iota(jnp.int32, shape, len(shape) - 2) < per

    def swap(a):
        return pltpu.roll(a, per, a.ndim - 2)

    def encode(total):
        high = total.astype(BF16).astype(F32)
        return jnp.where(is_re(total.shape), high, total - high)

    def decode(pair):
        return pair + swap(pair)

    def lanes(a):
        return jnp.broadcast_to(a, a.shape[:-1] + (LANES,))

    def event_of(k, shape):
        zl = lax.rem(lax.broadcasted_iota(jnp.int32, shape, 1), per)
        return (k * per + zl) * ny + lax.broadcasted_iota(jnp.int32, shape, 0)

    n_events = alpha_ref.shape[-1]

    def spread(ref, k):
        shape = (ny, PART, n_events)
        lane = lax.broadcasted_iota(jnp.int32, shape, 2)
        row = jnp.broadcast_to(ref[...].reshape(1, 1, n_events), shape)
        return lanes(jnp.sum(jnp.where(lane == event_of(k, shape), row, 0.0), axis=-1, keepdims=True))

    alpha = [spread(alpha_ref, k) for k in range(groups)]
    rho = [spread(rho_ref, k) for k in range(groups)]
    phi = [spread(phi_ref, k) for k in range(groups)]

    pl.semaphore_wait(barrier, len(peers))

    for d in range(grid.nz - 1, 0, -1):
        remote(first.at[z], first.at[z], first_send, first_recv, at_sta(lax.rem(z + d, grid.nz), y))
    for load in g_loads:
        load.wait()
    wait_bytes(first.at[pl.ds(0, grid.nz - 1)], first_recv)

    def share_y(t, k, q):
        here = vall.at[t, k, y, q]
        for d in y_order:
            remote(here, here, send.at[t, k, S_B5], recv.at[t, k, S_B5], at_sta(z, y_peer(d)))

    for k in range(groups):
        for e in range(per):
            block = first[k * per + e].astype(F32)
            for p in range(2):
                for q in range(nq):
                    first_rows[k, q, p * per + e : p * per + e + 1, :] = block[p * nq + q : p * nq + q + 1, :]
        vall[0, k, y, :, :, 0:width] = first_rows[k].astype(BF16)
        for q in range(nq):
            share_y(0, k, q)

    def columns(t, k, q):
        return vall[t, k, :, q, :, 0:width].astype(F32)

    def beta_squares(t, k):
        return decode(vall[t, k, :, 0, :, width:].astype(F32))

    def root(total, count):
        return jnp.sqrt(total * (1.0 / count) + EPS)

    def squares_of(values):
        total = jnp.sum(values[0] * values[0], axis=-1, keepdims=True)
        for value in values[1:]:
            total += jnp.sum(value * value, axis=-1, keepdims=True)
        total = lanes(total)
        return total + swap(total)

    contract = (((1,), (1,)), ((), ()))

    def stage_a1(t, k):
        wait_bytes(vall.at[t, k, pl.ds(0, ny - 1)], recv.at[t, k, S_B5])
        values = [columns(t, k, q) for q in range(nq)]
        product = jnp.zeros((ny * PART, 2 * rows_half), F32)
        for q in range(nq):
            left = values[q].reshape(ny * PART, width).astype(BF16)
            product += lax.dot_general(left, gmat[q], contract, preferred_element_type=F32)
        product = product.reshape(ny, PART, 2 * rows_half)
        turned = swap(product[..., rows_half:])
        image = product[..., :rows_half] + jnp.where(is_re(turned.shape), -turned, turned)
        if t == 0:
            scalars = jnp.zeros((ny, PART, LANES), F32)
            shape = image.shape
            event = event_of(k, shape)
            part_re = is_re(shape)
            per_src = station_ref.shape[1]
            for n in range(per_src):
                both = jnp.where(part_re, jnp.broadcast_to(station_ref[0, n : n + 1, :][None], shape),
                                 jnp.broadcast_to(station_ref[1, n : n + 1, :][None], shape))
                image -= jnp.where(event == src * per_src + n, alpha[k] * both, 0.0)
        else:
            scalars = encode(squares_of(values))
        message = jnp.concatenate([image, scalars], axis=-1).astype(BF16)
        for c in range(2):
            a1_out[t, k, c] = message[c * half_rows : (c + 1) * half_rows]
        a1_in[t, k, xc] = a1_out[t, k, core]
        for d in range(1, nxc):
            to = lax.rem(xc + d, nxc)
            remote(a1_out.at[t, k, lax.rem(to, 2)], a1_in.at[t, k, xc], send.at[t, k, S_A1], recv.at[t, k, S_A1],
                   at_src(zh * nxc + to))

    other = (1 - zh) * nxc + xc - core

    def stage_a2(t, k):
        wait_bytes(a1_in.at[t, k, pl.ds(0, nxc - 1)], recv.at[t, k, S_A1])
        total = a1_in[t, k, 0].astype(F32)
        for i in range(1, nxc):
            total += a1_in[t, k, i].astype(F32)
        scalars = encode(decode(total[..., rows_half:]))
        a2_in[t, k, zh * 2 + core] = jnp.concatenate([total[..., :rows_half], scalars], axis=-1).astype(BF16)
        here = a2_in.at[t, k, zh * 2 + core]
        for to in (other + core, other + 1 - core, src + 1 - 2 * core):
            remote(here, here, send.at[t, k, S_A2], recv.at[t, k, S_A2], at_src(to))

    def stage_a3(t, k):
        wait_bytes(a2_in.at[t, k, pl.ds(0, 3)], recv.at[t, k, S_A2])
        total = jnp.concatenate(
            [a2_in[t, k, c].astype(F32) + a2_in[t, k, 2 + c].astype(F32) for c in range(2)], axis=0)
        vector = total[..., :rows_half]
        if t > 0:
            alpha[k] = root(decode(total[..., rows_half:]), cols_total)
            beta = root(beta_squares(t, k), rows_total)
            vector = vector / alpha[k] - alpha[k] * (uhat[k] / beta)
        uhat[k] = vector
        scalars = encode(squares_of([vector])).astype(BF16)
        turned = swap(vector)
        left = jnp.concatenate([vector, jnp.where(is_re(turned.shape), turned, -turned)], axis=-1)
        left = left.reshape(ny * PART, 2 * rows_half).astype(BF16)
        for i in range(nq):
            q = by_distance(i, True)
            back = jnp.dot(left, gmat[q], preferred_element_type=F32)
            b1_out[t, k, :, q, :, 0:width] = back.reshape(ny, PART, width).astype(BF16)
            b1_out[t, k, :, q, :, width:] = scalars
            for d in y_order:
                remote(b1_out.at[t, k, y_peer(d), q], b1_in.at[t, k, q, y], send.at[t, k, S_B1],
                       recv.at[t, k, S_B1 + q], at_sta(z, y_peer(d)))

    def stage_b2(t, k):
        for i in range(nq):
            q = by_distance(i, True)
            wait_bytes(b1_in.at[t, k, q, pl.ds(0, ny - 1)], recv.at[t, k, S_B1 + q])
            total = b1_out[t, k, y, q].astype(F32)
            for d in range(1, ny):
                total += b1_in[t, k, q, y_peer(d)].astype(F32)
            b2_out[t, k, q, :, 0:width] = total[..., :width].astype(BF16)
            b2_out[t, k, q, :, width:] = encode(decode(total[..., width:])).astype(BF16)
            if i < nq - 1:
                remote(b2_out.at[t, k, q], b2_in.at[t, k, quad], send.at[t, k, S_B2], recv.at[t, k, S_B2],
                       at_sta(zhalf * nq + q, y))

    def stage_b3(t, k):
        wait_bytes(b2_in.at[t, k, pl.ds(0, nq - 1)], recv.at[t, k, S_B2])
        total = b2_out[t, k, quad].astype(F32)
        for d in range(1, nq):
            total += b2_in[t, k, lax.rem(quad + d, nq)].astype(F32)
        b3_out[t, k, :, 0:width] = total[:, :width].astype(BF16)
        b3_out[t, k, :, width:] = encode(decode(total[:, width:])).astype(BF16)
        remote(b3_out.at[t, k], b3_in.at[t, k], send.at[t, k, S_B3], recv.at[t, k, S_B3],
               at_sta((1 - zhalf) * nq + quad, y))

    def stage_b4(t, k):
        wait_bytes(b3_in.at[t, k], recv.at[t, k, S_B3])
        total = b3_out[t, k].astype(F32) + b3_in[t, k].astype(F32)
        squares = decode(total[:, width:])
        beta = root(squares, rows_total)[:, 0:1]
        before = vall[t, k, y, quad, :, 0:width].astype(F32)
        if t > 0:
            before = before / coef[k, 0, y][:, 0:1]
        after = total[:, :width] * (ratio / beta) - beta * before
        after = after.astype(BF16)
        if t == ITERS - 1:
            after32 = after.astype(F32)
            lane = lax.broadcasted_iota(jnp.int32, squares.shape, 1)
            slot = y * nq + quad
            fs1[k, slot] = jnp.where(lane < LANES // 2, squares_of([after32]), squares)
            for d in range(ny - 1, -1, -1):
                for e in range(nq):
                    if d or e:
                        remote(fs1.at[k, slot], fs1.at[k, slot], send.at[t + 1, k, 0], recv.at[t + 1, k, 0],
                               at_sta(zhalf * nq + lax.rem(quad + e, nq), y_peer(d)))
        vall[t + 1, k, y, quad, :, 0:width] = after
        vall[t + 1, k, y, quad, :, width:] = encode(squares).astype(BF16)
        here = vall.at[t + 1, k, y, quad]
        for i in range(nq - 1):
            to = by_distance(i, True)
            remote(here, here, send.at[t, k, S_B4], recv.at[t, k, S_B4 + quad], at_sta(zhalf * nq + to, y))
        if t < ITERS - 1:
            share_y(t + 1, k, quad)

    def stage_b5(t, k):
        for i in range(1, nq):
            q = by_distance(i, False)
            wait_bytes(vall.at[t + 1, k, y, q], recv.at[t, k, S_B4 + q])
            if t < ITERS - 1:
                share_y(t + 1, k, q)

    mine_k = lax.div(z, per)
    mine_row = lax.rem(z, per)

    def rotate(k, beta):
        rho_new = jnp.sqrt(rho[k] * rho[k] + beta * beta)
        cosine = rho[k] / rho_new
        sine = beta / rho_new
        coef[k, 0] = alpha[k]
        coef[k, 1] = cosine * phi[k] / rho_new
        coef[k, 2] = sine * alpha[k] / rho_new
        rho[k] = -cosine * alpha[k]
        phi[k] = sine * phi[k]

    def own_rows(t):
        block = vall[t, mine_k, y].astype(F32)[:, :, 0:width]
        row = lax.broadcasted_iota(jnp.int32, block.shape, 1)
        result = []
        for p in range(2):
            picked = jnp.sum(jnp.where(row == p * per + mine_row, block, 0.0), axis=1, keepdims=True)
            result.append(jnp.concatenate([picked[q] for q in range(nq)], axis=-1))
        return result

    def step(t, rows):
        def scalar(i):
            return coef[mine_k, i, y, pl.ds(mine_row, 1), :][:, 0:1]

        alpha_own, step_sol, step_dir = scalar(0), scalar(1), scalar(2)
        for p in range(2):
            vector = rows[p] / alpha_own
            before = search_out[p]
            sol_out[p] = sol_out[p] + step_sol * before
            search_out[p] = vector - step_dir * before
            if t == ITERS:
                source_out[p] = vector

    for t in range(ITERS):
        for k in range(groups):
            stage_a1(t, k)
        for k in range(groups):
            stage_a2(t, k)
        for k in range(groups):
            stage_a3(t, k)
        if t > 0:
            for k in range(groups):
                rotate(k, root(beta_squares(t, k), rows_total))
            step(t, own_rows(t))
        for stage in (stage_b2, stage_b3, stage_b4, stage_b5):
            for k in range(groups):
                stage(t, k)

    row = lax.broadcasted_iota(jnp.int32, (PART, LANES), 0)
    lane = lax.broadcasted_iota(jnp.int32, (PART, LANES), 1)
    seg = LANES // ny
    squares = jnp.zeros((PART, LANES), F32)
    betas = []
    for k in range(groups):
        wait_bytes(fs1.at[k, pl.ds(0, ny * nq - 1)], recv.at[ITERS, k, 0])
        beta_rows = []
        for i in range(ny):
            total = fs1[k, i * nq]
            beta_rows.append(lanes(total[:, LANES // 2 : LANES // 2 + 1]))
            for q in range(1, nq):
                total += fs1[k, i * nq + q]
            squares = jnp.where((lax.div(lane, seg) == i) & (lax.div(row, per) == k), lanes(total[:, 0:1]), squares)
        betas.append(root(jnp.stack(beta_rows), rows_total))
    fs2[src] = squares
    for d in range(1, n_src):
        remote(fs2.at[src], fs2.at[src], send.at[ITERS, 0, 1], recv.at[ITERS, 0, 1],
               at_src(lax.rem(src + d, n_src)))

    for k in range(groups):
        unorm[k] = uhat[k] / betas[k]
    per_src = station_ref.shape[1]
    for n in range(per_src):
        event = src * per_src + n
        at_y, at_z = lax.rem(event, ny), lax.div(event, ny)
        for p in range(2):
            station_out[p, n : n + 1, :] = unorm[
                lax.div(at_z, per), at_y, pl.ds(p * per + lax.rem(at_z, per), 1), :]
    last_rows = own_rows(ITERS)

    wait_bytes(fs2.at[pl.ds(0, n_src - 1)], recv.at[ITERS, 0, 1])
    squares = fs2[0]
    for i in range(1, n_src):
        squares += fs2[i]
    for k in range(groups):
        kept = jnp.where(lax.div(row, per) == k, squares, 0.0)
        kept = kept + swap(kept)
        alpha[k] = root(jnp.stack([lanes(kept[:, i * seg : i * seg + 1]) for i in range(ny)]), cols_total)
        rotate(k, betas[k])
    step(ITERS, last_rows)

    def collect(values):
        shape = (ny, PART, n_events)
        lane = lax.broadcasted_iota(jnp.int32, shape, 2)
        total = jnp.zeros((1, n_events), F32)
        for k in range(groups):
            keep = (lane == event_of(k, shape)) & is_re(shape)
            kept = jnp.where(keep, values[k][..., 0:1], 0.0).reshape(ny * PART, n_events)
            total += jnp.sum(kept, axis=0, keepdims=True)
        return total

    alpha_out[...] = collect(alpha)
    rho_out[...] = collect(rho)
    phi_out[...] = collect(phi)

    wait_bytes(first.at[pl.ds(0, grid.nz - 1)], first_send)
    wait_bytes(fs2.at[pl.ds(0, n_src - 1)], send.at[ITERS, 0, 1])
    for k in range(groups):
        wait_bytes(fs1.at[k, pl.ds(0, ny * nq - 1)], send.at[ITERS, k, 0])
        for t in range(ITERS):
            wait_bytes(a1_in.at[t, k, pl.ds(0, nxc - 1)], send.at[t, k, S_A1])
            wait_bytes(a2_in.at[t, k, pl.ds(0, 3)], send.at[t, k, S_A2])
            wait_bytes(vall.at[t, k, pl.ds(0, ny - 1)], send.at[t, k, S_B5])
            wait_bytes(b1_out.at[t, k, pl.ds(0, ny - 1)], send.at[t, k, S_B1])
            wait_bytes(b2_in.at[t, k, pl.ds(0, nq - 1)], send.at[t, k, S_B2])
            wait_bytes(b3_in.at[t, k], send.at[t, k, S_B3])
            wait_bytes(vall.at[t, k, 0, pl.ds(0, nq - 1)], send.at[t, k, S_B4])


def deliver(n, *refs):
    copies = [pltpu.make_async_copy(refs[i], refs[n + i], refs[2 * n].at[i]) for i in range(n)]
    for copy in copies:
        copy.start()
    for copy in copies:
        copy.wait()


def shards(grid, *args):
    green_real, station, source = args[0], args[2], args[3]
    rows = green_real.shape[0]
    rows_total = rows * lax.axis_size("sta")
    cols_total = green_real.shape[1] * lax.axis_size("src")
    ny, nq, groups = grid.ny, grid.nq, grid.groups
    width = green_real.shape[1] // nq
    padded = width + LANES
    n_events = args[6].shape[0]
    args = list(args[:6]) + [a.reshape(1, n_events) for a in args[6:]]
    vmem = pl.BlockSpec(memory_space=pltpu.VMEM)
    hbm = pl.BlockSpec(memory_space=pltpu.HBM)
    half = ny // 2
    message = rows + LANES

    def buf(*shape, kind=BF16):
        return pltpu.VMEM(shape, kind)

    scratch = [
        buf(*station.shape, kind=F32),
        buf(*source.shape, kind=F32),
        buf(1, n_events, kind=F32),
        buf(1, n_events, kind=F32),
        buf(1, n_events, kind=F32),
        buf(nq, 2 * rows, width),
        buf(grid.nz, 2 * nq, width),
        buf(groups, nq, PART, width, kind=F32),
        buf(ITERS + 1, groups, ny, nq, PART, padded),
        buf(ITERS, groups, 2, half, PART, message),
        buf(ITERS, groups, grid.nxc, half, PART, message),
        buf(ITERS, groups, 4, half, PART, message),
        buf(groups, ny * nq, PART, LANES, kind=F32),
        buf(grid.nzh * grid.nxc, PART, LANES, kind=F32),
        buf(ITERS, groups, ny, nq, PART, padded),
        buf(ITERS, groups, nq, ny, PART, padded),
        buf(ITERS, groups, nq, PART, padded),
        buf(ITERS, groups, nq, PART, padded),
        buf(ITERS, groups, PART, padded),
        buf(ITERS, groups, PART, padded),
        buf(groups, ny, PART, rows, kind=F32),
        buf(groups, ny, PART, rows, kind=F32),
        buf(groups, 3, ny, PART, LANES, kind=F32),
        pltpu.SemaphoreType.DMA((7 + 2 * nq,)),
        pltpu.SemaphoreType.DMA,
        pltpu.SemaphoreType.DMA,
        pltpu.SemaphoreType.DMA((ITERS + 1, groups, 5 + 2 * nq)),
        pltpu.SemaphoreType.DMA((ITERS + 1, groups, 5 + 2 * nq)),
    ]
    shapes = [station.shape, source.shape, source.shape, source.shape] + [(1, n_events)] * 3
    shapes = [jax.ShapeDtypeStruct(shape, F32) for shape in shapes]
    outs = pl.pallas_call(
        functools.partial(kernel, grid, rows_total, cols_total),
        out_shape=shapes,
        in_specs=[hbm] * 9,
        out_specs=[vmem] * 7,
        scratch_shapes=scratch,
        compiler_params=pltpu.CompilerParams(
            collective_id=0, has_side_effects=True),
        name="lsqr",
    )(*args)
    outs = pl.pallas_call(
        functools.partial(deliver, len(outs)),
        out_shape=shapes,
        in_specs=[vmem] * 7,
        out_specs=[hbm] * 7,
        scratch_shapes=[pltpu.SemaphoreType.DMA((7,))],
        name="deliver",
    )(*outs)
    return tuple(outs[:4]) + tuple(a.reshape(n_events) for a in outs[4:])


def build(mesh, grid):
    placed = (
        P("sta", "src"),
        P("sta", "src"),
        P(None, "src", "sta"),
        P(None, "sta", "src"),
        P(None, "sta", "src"),
        P(None, "sta", "src"),
        P(),
        P(),
        P(),
    )
    return jax.shard_map(
        functools.partial(shards, grid),
        mesh=mesh,
        in_specs=placed,
        out_specs=placed[2:],
        check_vma=False,
    )


def solution(mesh):
    return build(mesh, FULL)
```

time: 150 us -> 136 us (0.907)
  local copies, waits for them, and re-layouts: 8.83 us -> 0 us
  Pallas kernels: 140 us -> 135 us
    unnamed x25 -> x0, local copies, waits for them, and re-layouts: 8.83 us -> none
    pallas_call x1, Pallas kernels: 140 us -> 133 us  [shards(): pl.pallas_call(functools.partial(kernel, grid, rows_total, cols_total), o...]
where the time goes in v2:
time: 136 us
  Pallas kernels  135 us (99%)
    pallas_call x1, Pallas kernels, shards(): pl.pallas_call(functools.partial(kernel, grid, rows_total, cols_total), o...  133 us

profile of v2, /device:TPU:1, one launch (start us, length us, event | category | flops | bytes accessed | tf_op | source)
XLA Modules:
  0.0 135.6 jit_solution(13277052021507852986)
XLA Ops:
  0.6 133.5 %lsqr.1 = (f32[2,2,128]{2,1,0:T(2,128)}, f32[2,1,2048]{2,1,0:T(1,128)}, f32[2,1,2048]{2,1,0:T(1,128)}, f32[2,1,2048]{2,1,0:T(1,128)}, f32[1,32]{1,0:T(1,128)}, /*index=5*/f32[1,32]{1,0:T(1,128)}, f32[1,32]{1,0:T(1,128)}) custom-call(bf16[128,2048]{1,0:T(8,128)(2,1)} %refs_0_.1, bf16[128,2048]{1,0:T(8,128)(2,1)} %refs_1_.1, f32[2,2,128]{2,1,0:T(2,128)} %refs_2_.1, ...), custom_call_target="tpu_custom_call" | custom-call | tf_op jit(solution)/shard_map/lsqr/pallas_call | solution.py:494
  134.1 1.5 %deliver.1 = (f32[2,2,128]{2,1,0:T(2,128)}, f32[2,1,2048]{2,1,0:T(1,128)}, f32[2,1,2048]{2,1,0:T(1,128)}, f32[2,1,2048]{2,1,0:T(1,128)}, f32[1,32]{1,0:T(1,128)}, /*index=5*/f32[1,32]{1,0:T(1,128)}, f32[1,32]{1,0:T(1,128)}) custom-call(f32[2,2,128]{2,1,0:T(2,128)} %get-tuple-element.21.refs_0_, f32[2,1,2048]{2,1,0:T(1,128)} %get-tuple-element.22.refs_1_, ...), custom_call_target="tpu_custom_call" | custom-call | tf_op jit(solution)/shard_map/deliver/pallas_call | solution.py:504

commit v3 on v2

--- a/solution.py
+++ b/solution.py
@@ -34,7 +34,7 @@
      station_out, source_out, search_out, sol_out, alpha_out, rho_out, phi_out,
      station_ref, source_ref, alpha_ref, rho_ref, phi_ref,
      gmat, first, first_rows, vall, a1_out, a1_in, a2_in, fs1, fs2,
-     b1_out, b1_in, b2_out, b2_in, b3_out, b3_in,
+     b1_out, b1_in, b1s_out, b1s_in, b2_out, b2_in, b3_out, b3_in, beta_sq,
      uhat, unorm, coef, load_sem, first_send, first_recv, send, recv) = refs
     ny, nq, nxc, groups, per = grid.ny, grid.nq, grid.nxc, grid.groups, grid.per
     n_src = grid.nzh * nxc
@@ -42,7 +42,7 @@
     rows_half = gmat.shape[1] // 2
     half_rows = ny // 2
     ratio = cols_total / rows_total
-    S_A1, S_A2, S_B2, S_B3, S_B5, S_B1 = 0, 1, 2, 3, 4, 5
+    S_A1, S_A2, S_B2, S_B3, S_B5, S_B1S, S_B5S, S_B1 = 0, 1, 2, 3, 4, 5, 6, 7
     S_B4 = S_B1 + nq
 
     sta = lax.axis_index("sta")
@@ -165,15 +165,15 @@
             for p in range(2):
                 for q in range(nq):
                     first_rows[k, q, p * per + e : p * per + e + 1, :] = block[p * nq + q : p * nq + q + 1, :]
-        vall[0, k, y, :, :, 0:width] = first_rows[k].astype(BF16)
+        vall[0, k, y] = first_rows[k].astype(BF16)
         for q in range(nq):
             share_y(0, k, q)
 
     def columns(t, k, q):
-        return vall[t, k, :, q, :, 0:width].astype(F32)
+        return vall[t, k, :, q].astype(F32)
 
     def beta_squares(t, k):
-        return decode(vall[t, k, :, 0, :, width:].astype(F32))
+        return beta_sq[t, k]
 
     def root(total, count):
         return jnp.sqrt(total * (1.0 / count) + EPS)
@@ -184,6 +184,18 @@
             total += jnp.sum(value * value, axis=-1, keepdims=True)
         total = lanes(total)
         return total + swap(total)
+
+    seg_a = LANES // half_rows
+
+    def pack(chunks):
+        tile = chunks[0]
+        lane = lax.broadcasted_iota(jnp.int32, tile.shape, 1)
+        for i in range(1, half_rows):
+            tile = jnp.where(lane >= i * seg_a, chunks[i], tile)
+        return tile
+
+    def unpack(tile):
+        return [lanes(tile[:, i * seg_a : i * seg_a + 1]) for i in range(half_rows)]
 
     contract = (((1,), (1,)), ((), ()))
 
@@ -209,9 +221,11 @@
                 image -= jnp.where(event == src * per_src + n, alpha[k] * both, 0.0)
         else:
             scalars = encode(squares_of(values))
-        message = jnp.concatenate([image, scalars], axis=-1).astype(BF16)
+        message = image.astype(BF16)
         for c in range(2):
-            a1_out[t, k, c] = message[c * half_rows : (c + 1) * half_rows]
+            cut = slice(c * half_rows, (c + 1) * half_rows)
+            a1_out[t, k, c, 0:half_rows] = message[cut]
+            a1_out[t, k, c, half_rows] = pack(scalars[cut]).astype(BF16)
         a1_in[t, k, xc] = a1_out[t, k, core]
         for d in range(1, nxc):
             to = lax.rem(xc + d, nxc)
@@ -225,53 +239,63 @@
         total = a1_in[t, k, 0].astype(F32)
         for i in range(1, nxc):
             total += a1_in[t, k, i].astype(F32)
-        scalars = encode(decode(total[..., rows_half:]))
-        a2_in[t, k, zh * 2 + core] = jnp.concatenate([total[..., :rows_half], scalars], axis=-1).astype(BF16)
+        a2_in[t, k, zh * 2 + core, 0:half_rows] = total[0:half_rows].astype(BF16)
+        a2_in[t, k, zh * 2 + core, half_rows] = encode(decode(total[half_rows])).astype(BF16)
         here = a2_in.at[t, k, zh * 2 + core]
         for to in (other + core, other + 1 - core, src + 1 - 2 * core):
             remote(here, here, send.at[t, k, S_A2], recv.at[t, k, S_A2], at_src(to))
 
     def stage_a3(t, k):
         wait_bytes(a2_in.at[t, k, pl.ds(0, 3)], recv.at[t, k, S_A2])
-        total = jnp.concatenate(
-            [a2_in[t, k, c].astype(F32) + a2_in[t, k, 2 + c].astype(F32) for c in range(2)], axis=0)
-        vector = total[..., :rows_half]
+        totals = [a2_in[t, k, c].astype(F32) + a2_in[t, k, 2 + c].astype(F32) for c in range(2)]
+        vector = jnp.concatenate([total[0:half_rows] for total in totals], axis=0)
         if t > 0:
-            alpha[k] = root(decode(total[..., rows_half:]), cols_total)
+            squares = [decode(total[half_rows]) for total in totals]
+            alpha[k] = root(jnp.stack(unpack(squares[0]) + unpack(squares[1])), cols_total)
+            wait_bytes(beta_sq.at[t, k, pl.ds(0, ny - 1)], recv.at[t, k, S_B5S])
             beta = root(beta_squares(t, k), rows_total)
             vector = vector / alpha[k] - alpha[k] * (uhat[k] / beta)
         uhat[k] = vector
-        scalars = encode(squares_of([vector])).astype(BF16)
+        b1s_out[t, k] = squares_of([vector])
         turned = swap(vector)
         left = jnp.concatenate([vector, jnp.where(is_re(turned.shape), turned, -turned)], axis=-1)
         left = left.reshape(ny * PART, 2 * rows_half).astype(BF16)
         for i in range(nq):
             q = by_distance(i, True)
             back = jnp.dot(left, gmat[q], preferred_element_type=F32)
-            b1_out[t, k, :, q, :, 0:width] = back.reshape(ny, PART, width).astype(BF16)
-            b1_out[t, k, :, q, :, width:] = scalars
+            b1_out[t, k, :, q] = back.reshape(ny, PART, width).astype(BF16)
+            if i == 0:
+                for d in y_order:
+                    remote(b1s_out.at[t, k, y_peer(d)], b1s_in.at[t, k, y], send.at[t, k, S_B1S],
+                           recv.at[t, k, S_B1S], at_sta(z, y_peer(d)))
             for d in y_order:
                 remote(b1_out.at[t, k, y_peer(d), q], b1_in.at[t, k, q, y], send.at[t, k, S_B1],
                        recv.at[t, k, S_B1 + q], at_sta(z, y_peer(d)))
 
     def stage_b2(t, k):
+        wait_bytes(b1s_in.at[t, k, pl.ds(0, ny - 1)], recv.at[t, k, S_B1S])
+        squares = b1s_out[t, k, y]
+        for d in range(1, ny):
+            squares += b1s_in[t, k, y_peer(d)]
+        squares = encode(squares).astype(BF16)
         for i in range(nq):
             q = by_distance(i, True)
             wait_bytes(b1_in.at[t, k, q, pl.ds(0, ny - 1)], recv.at[t, k, S_B1 + q])
             total = b1_out[t, k, y, q].astype(F32)
             for d in range(1, ny):
                 total += b1_in[t, k, q, y_peer(d)].astype(F32)
-            b2_out[t, k, q, :, 0:width] = total[..., :width].astype(BF16)
-            b2_out[t, k, q, :, width:] = encode(decode(total[..., width:])).astype(BF16)
+            b2_out[t, k, q, :, 0:width] = total.astype(BF16)
+            b2_out[t, k, q, :, width:] = squares
             if i < nq - 1:
                 remote(b2_out.at[t, k, q], b2_in.at[t, k, quad], send.at[t, k, S_B2], recv.at[t, k, S_B2],
                        at_sta(zhalf * nq + q, y))
 
     def stage_b3(t, k):
         wait_bytes(b2_in.at[t, k, pl.ds(0, nq - 1)], recv.at[t, k, S_B2])
-        total = b2_out[t, k, quad].astype(F32)
-        for d in range(1, nq):
-            total += b2_in[t, k, lax.rem(quad + d, nq)].astype(F32)
+        b2_in[t, k, quad] = b2_out[t, k, quad]
+        total = b2_in[t, k, 0].astype(F32)
+        for i in range(1, nq):
+            total += b2_in[t, k, i].astype(F32)
         b3_out[t, k, :, 0:width] = total[:, :width].astype(BF16)
         b3_out[t, k, :, width:] = encode(decode(total[:, width:])).astype(BF16)
         remote(b3_out.at[t, k], b3_in.at[t, k], send.at[t, k, S_B3], recv.at[t, k, S_B3],
@@ -282,7 +306,7 @@
         total = b3_out[t, k].astype(F32) + b3_in[t, k].astype(F32)
         squares = decode(total[:, width:])
         beta = root(squares, rows_total)[:, 0:1]
-        before = vall[t, k, y, quad, :, 0:width].astype(F32)
+        before = vall[t, k, y, quad].astype(F32)
         if t > 0:
             before = before / coef[k, 0, y][:, 0:1]
         after = total[:, :width] * (ratio / beta) - beta * before
@@ -297,14 +321,17 @@
                     if d or e:
                         remote(fs1.at[k, slot], fs1.at[k, slot], send.at[t + 1, k, 0], recv.at[t + 1, k, 0],
                                at_sta(zhalf * nq + lax.rem(quad + e, nq), y_peer(d)))
-        vall[t + 1, k, y, quad, :, 0:width] = after
-        vall[t + 1, k, y, quad, :, width:] = encode(squares).astype(BF16)
+        vall[t + 1, k, y, quad] = after
         here = vall.at[t + 1, k, y, quad]
         for i in range(nq - 1):
             to = by_distance(i, True)
             remote(here, here, send.at[t, k, S_B4], recv.at[t, k, S_B4 + quad], at_sta(zhalf * nq + to, y))
         if t < ITERS - 1:
             share_y(t + 1, k, quad)
+            beta_sq[t + 1, k, y] = squares
+            for d in y_order:
+                remote(beta_sq.at[t + 1, k, y], beta_sq.at[t + 1, k, y], send.at[t + 1, k, S_B5S],
+                       recv.at[t + 1, k, S_B5S], at_sta(z, y_peer(d)))
 
     def stage_b5(t, k):
         for i in range(1, nq):
@@ -327,7 +354,7 @@
         phi[k] = sine * phi[k]
 
     def own_rows(t):
-        block = vall[t, mine_k, y].astype(F32)[:, :, 0:width]
+        block = vall[t, mine_k, y].astype(F32)
         row = lax.broadcasted_iota(jnp.int32, block.shape, 1)
         result = []
         for p in range(2):
@@ -431,6 +458,9 @@
             wait_bytes(b2_in.at[t, k, pl.ds(0, nq - 1)], send.at[t, k, S_B2])
             wait_bytes(b3_in.at[t, k], send.at[t, k, S_B3])
             wait_bytes(vall.at[t, k, 0, pl.ds(0, nq - 1)], send.at[t, k, S_B4])
+            wait_bytes(b1s_in.at[t, k, pl.ds(0, ny - 1)], send.at[t, k, S_B1S])
+            if t > 0:
+                wait_bytes(beta_sq.at[t, k, pl.ds(0, ny - 1)], send.at[t, k, S_B5S])
 
 
 def deliver(n, *refs):
@@ -454,7 +484,6 @@
     vmem = pl.BlockSpec(memory_space=pltpu.VMEM)
     hbm = pl.BlockSpec(memory_space=pltpu.HBM)
     half = ny // 2
-    message = rows + LANES
 
     def buf(*shape, kind=BF16):
         return pltpu.VMEM(shape, kind)
@@ -468,26 +497,29 @@
         buf(nq, 2 * rows, width),
         buf(grid.nz, 2 * nq, width),
         buf(groups, nq, PART, width, kind=F32),
-        buf(ITERS + 1, groups, ny, nq, PART, padded),
-        buf(ITERS, groups, 2, half, PART, message),
-        buf(ITERS, groups, grid.nxc, half, PART, message),
-        buf(ITERS, groups, 4, half, PART, message),
+        buf(ITERS + 1, groups, ny, nq, PART, width),
+        buf(ITERS, groups, 2, half + 1, PART, LANES),
+        buf(ITERS, groups, grid.nxc, half + 1, PART, LANES),
+        buf(ITERS, groups, 4, half + 1, PART, LANES),
         buf(groups, ny * nq, PART, LANES, kind=F32),
         buf(grid.nzh * grid.nxc, PART, LANES, kind=F32),
-        buf(ITERS, groups, ny, nq, PART, padded),
-        buf(ITERS, groups, nq, ny, PART, padded),
+        buf(ITERS, groups, ny, nq, PART, width),
+        buf(ITERS, groups, nq, ny, PART, width),
+        buf(ITERS, groups, ny, PART, LANES, kind=F32),
+        buf(ITERS, groups, ny, PART, LANES, kind=F32),
         buf(ITERS, groups, nq, PART, padded),
         buf(ITERS, groups, nq, PART, padded),
         buf(ITERS, groups, PART, padded),
         buf(ITERS, groups, PART, padded),
+        buf(ITERS, groups, ny, PART, LANES, kind=F32),
         buf(groups, ny, PART, rows, kind=F32),
         buf(groups, ny, PART, rows, kind=F32),
         buf(groups, 3, ny, PART, LANES, kind=F32),
         pltpu.SemaphoreType.DMA((7 + 2 * nq,)),
         pltpu.SemaphoreType.DMA,
         pltpu.SemaphoreType.DMA,
-        pltpu.SemaphoreType.DMA((ITERS + 1, groups, 5 + 2 * nq)),
-        pltpu.SemaphoreType.DMA((ITERS + 1, groups, 5 + 2 * nq)),
+        pltpu.SemaphoreType.DMA((ITERS + 1, groups, 7 + 2 * nq)),
+        pltpu.SemaphoreType.DMA((ITERS + 1, groups, 7 + 2 * nq)),
     ]
     shapes = [station.shape, source.shape, source.shape, source.shape] + [(1, n_events)] * 3
     shapes = [jax.ShapeDtypeStruct(shape, F32) for shape in shapes]

time: 136 us -> 135 us (level)
  no operation moved by 1% of the time
where the time goes in v3:
time: 135 us
  Pallas kernels  134 us (99%)
    pallas_call x1, Pallas kernels, shards(): pl.pallas_call(functools.partial(kernel, grid, rows_total, cols_total), o...  133 us

profile of v3, /device:TPU:1, one launch (start us, length us, event | category | flops | bytes accessed | tf_op | source)
XLA Modules:
  0.0 135.1 jit_solution(6271008817697850574)
XLA Ops:
  0.6 133.0 %lsqr.1 = (f32[2,2,128]{2,1,0:T(2,128)}, f32[2,1,2048]{2,1,0:T(1,128)}, f32[2,1,2048]{2,1,0:T(1,128)}, f32[2,1,2048]{2,1,0:T(1,128)}, f32[1,32]{1,0:T(1,128)}, /*index=5*/f32[1,32]{1,0:T(1,128)}, f32[1,32]{1,0:T(1,128)}) custom-call(bf16[128,2048]{1,0:T(8,128)(2,1)} %refs_0_.1, bf16[128,2048]{1,0:T(8,128)(2,1)} %refs_1_.1, f32[2,2,128]{2,1,0:T(2,128)} %refs_2_.1, ...), custom_call_target="tpu_custom_call" | custom-call | tf_op jit(solution)/shard_map/lsqr/pallas_call | solution.py:526
  133.7 1.5 %deliver.1 = (f32[2,2,128]{2,1,0:T(2,128)}, f32[2,1,2048]{2,1,0:T(1,128)}, f32[2,1,2048]{2,1,0:T(1,128)}, f32[2,1,2048]{2,1,0:T(1,128)}, f32[1,32]{1,0:T(1,128)}, /*index=5*/f32[1,32]{1,0:T(1,128)}, f32[1,32]{1,0:T(1,128)}) custom-call(f32[2,2,128]{2,1,0:T(2,128)} %get-tuple-element.21.refs_0_, f32[2,1,2048]{2,1,0:T(1,128)} %get-tuple-element.22.refs_1_, ...), custom_call_target="tpu_custom_call" | custom-call | tf_op jit(solution)/shard_map/deliver/pallas_call | solution.py:536

commit v4 on v3

--- a/solution.py
+++ b/solution.py
@@ -34,7 +34,7 @@
      station_out, source_out, search_out, sol_out, alpha_out, rho_out, phi_out,
      station_ref, source_ref, alpha_ref, rho_ref, phi_ref,
      gmat, first, first_rows, vall, a1_out, a1_in, a2_in, fs1, fs2,
-     b1_out, b1_in, b1s_out, b1s_in, b2_out, b2_in, b3_out, b3_in, beta_sq,
+     b1_out, b1_in, b3_out, b3_in, beta_sq,
      uhat, unorm, coef, load_sem, first_send, first_recv, send, recv) = refs
     ny, nq, nxc, groups, per = grid.ny, grid.nq, grid.nxc, grid.groups, grid.per
     n_src = grid.nzh * nxc
@@ -42,8 +42,8 @@
     rows_half = gmat.shape[1] // 2
     half_rows = ny // 2
     ratio = cols_total / rows_total
-    S_A1, S_A2, S_B2, S_B3, S_B5, S_B1S, S_B5S, S_B1 = 0, 1, 2, 3, 4, 5, 6, 7
-    S_B4 = S_B1 + nq
+    S_A1, S_A2, S_B1, S_B3, S_V, S_BETA, S_LAST = range(7)
+    n_own = ny * nq
 
     sta = lax.axis_index("sta")
     src = lax.axis_index("src")
@@ -154,23 +154,23 @@
         load.wait()
     wait_bytes(first.at[pl.ds(0, grid.nz - 1)], first_recv)
 
-    def share_y(t, k, q):
-        here = vall.at[t, k, y, q]
-        for d in y_order:
-            remote(here, here, send.at[t, k, S_B5], recv.at[t, k, S_B5], at_sta(z, y_peer(d)))
-
     for k in range(groups):
         for e in range(per):
             block = first[k * per + e].astype(F32)
             for p in range(2):
                 for q in range(nq):
                     first_rows[k, q, p * per + e : p * per + e + 1, :] = block[p * nq + q : p * nq + q + 1, :]
-        vall[0, k, y] = first_rows[k].astype(BF16)
-        for q in range(nq):
-            share_y(0, k, q)
+        mine = pl.ds(y * nq, nq)
+        vall[0, k, mine] = first_rows[k].astype(BF16)
+        for d in y_order:
+            remote(vall.at[0, k, mine], vall.at[0, k, mine], send.at[0, k, S_V], recv.at[0, k, S_V],
+                   at_sta(z, y_peer(d)))
+
+    def blocks_in(t):
+        return n_own - (nq if t == 0 else 1)
 
     def columns(t, k, q):
-        return vall[t, k, :, q].astype(F32)
+        return jnp.stack([vall[t, k, i * nq + q].astype(F32) for i in range(ny)])
 
     def beta_squares(t, k):
         return beta_sq[t, k]
@@ -199,8 +199,10 @@
 
     contract = (((1,), (1,)), ((), ()))
 
+    slot = y * nq + quad
+
     def stage_a1(t, k):
-        wait_bytes(vall.at[t, k, pl.ds(0, ny - 1)], recv.at[t, k, S_B5])
+        wait_bytes(vall.at[t, k, pl.ds(0, blocks_in(t))], recv.at[t, k, S_V])
         values = [columns(t, k, q) for q in range(nq)]
         product = jnp.zeros((ny * PART, 2 * rows_half), F32)
         for q in range(nq):
@@ -252,93 +254,69 @@
         if t > 0:
             squares = [decode(total[half_rows]) for total in totals]
             alpha[k] = root(jnp.stack(unpack(squares[0]) + unpack(squares[1])), cols_total)
-            wait_bytes(beta_sq.at[t, k, pl.ds(0, ny - 1)], recv.at[t, k, S_B5S])
+            wait_bytes(beta_sq.at[t, k, pl.ds(0, ny - 1)], recv.at[t, k, S_BETA])
             beta = root(beta_squares(t, k), rows_total)
             vector = vector / alpha[k] - alpha[k] * (uhat[k] / beta)
         uhat[k] = vector
-        b1s_out[t, k] = squares_of([vector])
+        scalars = encode(squares_of([vector])).astype(BF16)
         turned = swap(vector)
         left = jnp.concatenate([vector, jnp.where(is_re(turned.shape), turned, -turned)], axis=-1)
         left = left.reshape(ny * PART, 2 * rows_half).astype(BF16)
         for i in range(nq):
             q = by_distance(i, True)
             back = jnp.dot(left, gmat[q], preferred_element_type=F32)
-            b1_out[t, k, :, q] = back.reshape(ny, PART, width).astype(BF16)
-            if i == 0:
-                for d in y_order:
-                    remote(b1s_out.at[t, k, y_peer(d)], b1s_in.at[t, k, y], send.at[t, k, S_B1S],
-                           recv.at[t, k, S_B1S], at_sta(z, y_peer(d)))
+            b1_out[t, k, q, :, :, 0:width] = back.reshape(ny, PART, width).astype(BF16)
+            b1_out[t, k, q, :, :, width:] = scalars
+            if i < nq - 1:
+                remote(b1_out.at[t, k, q, y], b1_in.at[t, k, slot], send.at[t, k, S_B1], recv.at[t, k, S_B1],
+                       at_sta(zhalf * nq + q, y))
             for d in y_order:
-                remote(b1_out.at[t, k, y_peer(d), q], b1_in.at[t, k, q, y], send.at[t, k, S_B1],
-                       recv.at[t, k, S_B1 + q], at_sta(z, y_peer(d)))
-
-    def stage_b2(t, k):
-        wait_bytes(b1s_in.at[t, k, pl.ds(0, ny - 1)], recv.at[t, k, S_B1S])
-        squares = b1s_out[t, k, y]
-        for d in range(1, ny):
-            squares += b1s_in[t, k, y_peer(d)]
-        squares = encode(squares).astype(BF16)
-        for i in range(nq):
-            q = by_distance(i, True)
-            wait_bytes(b1_in.at[t, k, q, pl.ds(0, ny - 1)], recv.at[t, k, S_B1 + q])
-            total = b1_out[t, k, y, q].astype(F32)
-            for d in range(1, ny):
-                total += b1_in[t, k, q, y_peer(d)].astype(F32)
-            b2_out[t, k, q, :, 0:width] = total.astype(BF16)
-            b2_out[t, k, q, :, width:] = squares
-            if i < nq - 1:
-                remote(b2_out.at[t, k, q], b2_in.at[t, k, quad], send.at[t, k, S_B2], recv.at[t, k, S_B2],
-                       at_sta(zhalf * nq + q, y))
+                remote(b1_out.at[t, k, q, y_peer(d)], b1_in.at[t, k, slot], send.at[t, k, S_B1],
+                       recv.at[t, k, S_B1], at_sta(zhalf * nq + q, y_peer(d)))
 
     def stage_b3(t, k):
-        wait_bytes(b2_in.at[t, k, pl.ds(0, nq - 1)], recv.at[t, k, S_B2])
-        b2_in[t, k, quad] = b2_out[t, k, quad]
-        total = b2_in[t, k, 0].astype(F32)
-        for i in range(1, nq):
-            total += b2_in[t, k, i].astype(F32)
+        b1_in[t, k, slot] = b1_out[t, k, quad, y]
+        wait_bytes(b1_in.at[t, k, pl.ds(0, n_own - 1)], recv.at[t, k, S_B1])
+        total = b1_in[t, k, 0].astype(F32)
+        for i in range(1, n_own):
+            total += b1_in[t, k, i].astype(F32)
         b3_out[t, k, :, 0:width] = total[:, :width].astype(BF16)
         b3_out[t, k, :, width:] = encode(decode(total[:, width:])).astype(BF16)
         remote(b3_out.at[t, k], b3_in.at[t, k], send.at[t, k, S_B3], recv.at[t, k, S_B3],
                at_sta((1 - zhalf) * nq + quad, y))
 
+    def to_half(ref, send_sem, recv_sem):
+        for i in range(nq):
+            q = by_distance(i, True)
+            for d in y_order + [0]:
+                if d or i < nq - 1:
+                    remote(ref, ref, send_sem, recv_sem, at_sta(zhalf * nq + q, y_peer(d)))
+
     def stage_b4(t, k):
+        before = vall[t, k, slot].astype(F32)
+        if t > 0:
+            before = before / coef[k, 0, y][:, 0:1]
         wait_bytes(b3_in.at[t, k], recv.at[t, k, S_B3])
         total = b3_out[t, k].astype(F32) + b3_in[t, k].astype(F32)
         squares = decode(total[:, width:])
         beta = root(squares, rows_total)[:, 0:1]
-        before = vall[t, k, y, quad].astype(F32)
-        if t > 0:
-            before = before / coef[k, 0, y][:, 0:1]
         after = total[:, :width] * (ratio / beta) - beta * before
         after = after.astype(BF16)
-        if t == ITERS - 1:
-            after32 = after.astype(F32)
-            lane = lax.broadcasted_iota(jnp.int32, squares.shape, 1)
-            slot = y * nq + quad
-            fs1[k, slot] = jnp.where(lane < LANES // 2, squares_of([after32]), squares)
-            for d in range(ny - 1, -1, -1):
-                for e in range(nq):
-                    if d or e:
-                        remote(fs1.at[k, slot], fs1.at[k, slot], send.at[t + 1, k, 0], recv.at[t + 1, k, 0],
-                               at_sta(zhalf * nq + lax.rem(quad + e, nq), y_peer(d)))
-        vall[t + 1, k, y, quad] = after
-        here = vall.at[t + 1, k, y, quad]
-        for i in range(nq - 1):
-            to = by_distance(i, True)
-            remote(here, here, send.at[t, k, S_B4], recv.at[t, k, S_B4 + quad], at_sta(zhalf * nq + to, y))
+        vall[t + 1, k, slot] = after
+        here = vall.at[t + 1, k, slot]
         if t < ITERS - 1:
-            share_y(t + 1, k, quad)
+            to_half(here, send.at[t + 1, k, S_V], recv.at[t + 1, k, S_V])
             beta_sq[t + 1, k, y] = squares
             for d in y_order:
-                remote(beta_sq.at[t + 1, k, y], beta_sq.at[t + 1, k, y], send.at[t + 1, k, S_B5S],
-                       recv.at[t + 1, k, S_B5S], at_sta(z, y_peer(d)))
-
-    def stage_b5(t, k):
-        for i in range(1, nq):
-            q = by_distance(i, False)
-            wait_bytes(vall.at[t + 1, k, y, q], recv.at[t, k, S_B4 + q])
-            if t < ITERS - 1:
-                share_y(t + 1, k, q)
+                remote(beta_sq.at[t + 1, k, y], beta_sq.at[t + 1, k, y], send.at[t + 1, k, S_BETA],
+                       recv.at[t + 1, k, S_BETA], at_sta(z, y_peer(d)))
+        else:
+            lane = lax.broadcasted_iota(jnp.int32, squares.shape, 1)
+            fs1[k, slot] = jnp.where(lane < LANES // 2, squares_of([after.astype(F32)]), squares)
+            to_half(fs1.at[k, slot], send.at[t + 1, k, 0], recv.at[t + 1, k, 0])
+            for i in range(nq - 1):
+                to = by_distance(i, True)
+                remote(here, here, send.at[t, k, S_LAST], recv.at[t, k, S_LAST], at_sta(zhalf * nq + to, y))
 
     mine_k = lax.div(z, per)
     mine_row = lax.rem(z, per)
@@ -354,7 +332,7 @@
         phi[k] = sine * phi[k]
 
     def own_rows(t):
-        block = vall[t, mine_k, y].astype(F32)
+        block = vall[t, mine_k, pl.ds(y * nq, nq)].astype(F32)
         row = lax.broadcasted_iota(jnp.int32, block.shape, 1)
         result = []
         for p in range(2):
@@ -386,7 +364,7 @@
             for k in range(groups):
                 rotate(k, root(beta_squares(t, k), rows_total))
             step(t, own_rows(t))
-        for stage in (stage_b2, stage_b3, stage_b4, stage_b5):
+        for stage in (stage_b3, stage_b4):
             for k in range(groups):
                 stage(t, k)
 
@@ -419,6 +397,8 @@
         for p in range(2):
             station_out[p, n : n + 1, :] = unorm[
                 lax.div(at_z, per), at_y, pl.ds(p * per + lax.rem(at_z, per), 1), :]
+    for k in range(groups):
+        wait_bytes(vall.at[ITERS, k, pl.ds(0, nq - 1)], recv.at[ITERS - 1, k, S_LAST])
     last_rows = own_rows(ITERS)
 
     wait_bytes(fs2.at[pl.ds(0, n_src - 1)], recv.at[ITERS, 0, 1])
@@ -453,14 +433,12 @@
         for t in range(ITERS):
             wait_bytes(a1_in.at[t, k, pl.ds(0, nxc - 1)], send.at[t, k, S_A1])
             wait_bytes(a2_in.at[t, k, pl.ds(0, 3)], send.at[t, k, S_A2])
-            wait_bytes(vall.at[t, k, pl.ds(0, ny - 1)], send.at[t, k, S_B5])
-            wait_bytes(b1_out.at[t, k, pl.ds(0, ny - 1)], send.at[t, k, S_B1])
-            wait_bytes(b2_in.at[t, k, pl.ds(0, nq - 1)], send.at[t, k, S_B2])
+            wait_bytes(vall.at[t, k, pl.ds(0, blocks_in(t))], send.at[t, k, S_V])
+            wait_bytes(b1_in.at[t, k, pl.ds(0, n_own - 1)], send.at[t, k, S_B1])
             wait_bytes(b3_in.at[t, k], send.at[t, k, S_B3])
-            wait_bytes(vall.at[t, k, 0, pl.ds(0, nq - 1)], send.at[t, k, S_B4])
-            wait_bytes(b1s_in.at[t, k, pl.ds(0, ny - 1)], send.at[t, k, S_B1S])
             if t > 0:
-                wait_bytes(beta_sq.at[t, k, pl.ds(0, ny - 1)], send.at[t, k, S_B5S])
+                wait_bytes(beta_sq.at[t, k, pl.ds(0, ny - 1)], send.at[t, k, S_BETA])
+        wait_bytes(vall.at[ITERS, k, pl.ds(0, nq - 1)], send.at[ITERS - 1, k, S_LAST])
 
 
 def deliver(n, *refs):
@@ -497,18 +475,14 @@
         buf(nq, 2 * rows, width),
         buf(grid.nz, 2 * nq, width),
         buf(groups, nq, PART, width, kind=F32),
-        buf(ITERS + 1, groups, ny, nq, PART, width),
+        buf(ITERS + 1, groups, ny * nq, PART, width),
         buf(ITERS, groups, 2, half + 1, PART, LANES),
         buf(ITERS, groups, grid.nxc, half + 1, PART, LANES),
         buf(ITERS, groups, 4, half + 1, PART, LANES),
         buf(groups, ny * nq, PART, LANES, kind=F32),
         buf(grid.nzh * grid.nxc, PART, LANES, kind=F32),
-        buf(ITERS, groups, ny, nq, PART, width),
-        buf(ITERS, groups, nq, ny, PART, width),
-        buf(ITERS, groups, ny, PART, LANES, kind=F32),
-        buf(ITERS, groups, ny, PART, LANES, kind=F32),
-        buf(ITERS, groups, nq, PART, padded),
-        buf(ITERS, groups, nq, PART, padded),
+        buf(ITERS, groups, nq, ny, PART, padded),
+        buf(ITERS, groups, ny * nq, PART, padded),
         buf(ITERS, groups, PART, padded),
         buf(ITERS, groups, PART, padded),
         buf(ITERS, groups, ny, PART, LANES, kind=F32),
@@ -518,8 +492,8 @@
         pltpu.SemaphoreType.DMA((7 + 2 * nq,)),
         pltpu.SemaphoreType.DMA,
         pltpu.SemaphoreType.DMA,
-        pltpu.SemaphoreType.DMA((ITERS + 1, groups, 7 + 2 * nq)),
-        pltpu.SemaphoreType.DMA((ITERS + 1, groups, 7 + 2 * nq)),
+        pltpu.SemaphoreType.DMA((ITERS + 1, groups, 7)),
+        pltpu.SemaphoreType.DMA((ITERS + 1, groups, 7)),
     ]
     shapes = [station.shape, source.shape, source.shape, source.shape] + [(1, n_events)] * 3
     shapes = [jax.ShapeDtypeStruct(shape, F32) for shape in shapes]

time: 135 us -> 134 us (level)
  no operation moved by 1% of the time
where the time goes in v4:
time: 134 us
  Pallas kernels  133 us (99%)
    pallas_call x1, Pallas kernels, shards(): pl.pallas_call(functools.partial(kernel, grid, rows_total, cols_total), o...  132 us

profile of v4, /device:TPU:1, one launch (start us, length us, event | category | flops | bytes accessed | tf_op | source)
XLA Modules:
  0.0 133.8 jit_solution(1967337072647397110)
XLA Ops:
  0.6 131.7 %lsqr.1 = (f32[2,2,128]{2,1,0:T(2,128)}, f32[2,1,2048]{2,1,0:T(1,128)}, f32[2,1,2048]{2,1,0:T(1,128)}, f32[2,1,2048]{2,1,0:T(1,128)}, f32[1,32]{1,0:T(1,128)}, /*index=5*/f32[1,32]{1,0:T(1,128)}, f32[1,32]{1,0:T(1,128)}) custom-call(bf16[128,2048]{1,0:T(8,128)(2,1)} %refs_0_.1, bf16[128,2048]{1,0:T(8,128)(2,1)} %refs_1_.1, f32[2,2,128]{2,1,0:T(2,128)} %refs_2_.1, ...), custom_call_target="tpu_custom_call" | custom-call | tf_op jit(solution)/shard_map/lsqr/pallas_call | solution.py:500
  132.3 1.5 %deliver.1 = (f32[2,2,128]{2,1,0:T(2,128)}, f32[2,1,2048]{2,1,0:T(1,128)}, f32[2,1,2048]{2,1,0:T(1,128)}, f32[2,1,2048]{2,1,0:T(1,128)}, f32[1,32]{1,0:T(1,128)}, /*index=5*/f32[1,32]{1,0:T(1,128)}, f32[1,32]{1,0:T(1,128)}) custom-call(f32[2,2,128]{2,1,0:T(2,128)} %get-tuple-element.21.refs_0_, f32[2,1,2048]{2,1,0:T(1,128)} %get-tuple-element.22.refs_1_, ...), custom_call_target="tpu_custom_call" | custom-call | tf_op jit(solution)/shard_map/deliver/pallas_call | solution.py:510

commit v5 on v4

--- a/solution.py
+++ b/solution.py
@@ -33,16 +33,15 @@
     (green_re, green_im, station_in, source_in, search_in, sol_in, alpha_in, rho_in, phi_in,
      station_out, source_out, search_out, sol_out, alpha_out, rho_out, phi_out,
      station_ref, source_ref, alpha_ref, rho_ref, phi_ref,
-     gmat, first, first_rows, vall, a1_out, a1_in, a2_in, fs1, fs2,
-     b1_out, b1_in, b3_out, b3_in, beta_sq,
+     gmat, first, first_rows, vall, a1_in, a2_in, fs1, fs2,
+     b1_out, b1_in, by_out, by_in, bq_in, b3_out, b3_in, beta_sq,
      uhat, unorm, coef, load_sem, first_send, first_recv, send, recv) = refs
     ny, nq, nxc, groups, per = grid.ny, grid.nq, grid.nxc, grid.groups, grid.per
     n_src = grid.nzh * nxc
     width = source_ref.shape[-1] // nq
     rows_half = gmat.shape[1] // 2
-    half_rows = ny // 2
     ratio = cols_total / rows_total
-    S_A1, S_A2, S_B1, S_B3, S_V, S_BETA, S_LAST = range(7)
+    S_A1, S_A2, S_B1, S_B3, S_V, S_BETA, S_LAST, S_BY, S_BQ = range(9)
     n_own = ny * nq
 
     sta = lax.axis_index("sta")
@@ -53,7 +52,6 @@
     zhalf = lax.div(z, nq)
     zh = lax.div(src, nxc)
     xc = lax.rem(src, nxc)
-    core = lax.rem(xc, 2)
 
     def at_sta(z_at, y_at):
         return {"sta": z_at * ny + y_at, "src": src}
@@ -185,17 +183,17 @@
         total = lanes(total)
         return total + swap(total)
 
-    seg_a = LANES // half_rows
+    seg = LANES // ny
 
     def pack(chunks):
         tile = chunks[0]
         lane = lax.broadcasted_iota(jnp.int32, tile.shape, 1)
-        for i in range(1, half_rows):
-            tile = jnp.where(lane >= i * seg_a, chunks[i], tile)
+        for i in range(1, ny):
+            tile = jnp.where(lane >= i * seg, chunks[i], tile)
         return tile
 
     def unpack(tile):
-        return [lanes(tile[:, i * seg_a : i * seg_a + 1]) for i in range(half_rows)]
+        return jnp.stack([lanes(tile[:, i * seg : i * seg + 1]) for i in range(ny)])
 
     contract = (((1,), (1,)), ((), ()))
 
@@ -223,50 +221,39 @@
                 image -= jnp.where(event == src * per_src + n, alpha[k] * both, 0.0)
         else:
             scalars = encode(squares_of(values))
-        message = image.astype(BF16)
-        for c in range(2):
-            cut = slice(c * half_rows, (c + 1) * half_rows)
-            a1_out[t, k, c, 0:half_rows] = message[cut]
-            a1_out[t, k, c, half_rows] = pack(scalars[cut]).astype(BF16)
-        a1_in[t, k, xc] = a1_out[t, k, core]
+        a1_in[t, k, xc, 0:ny] = image.astype(BF16)
+        a1_in[t, k, xc, ny] = pack(scalars).astype(BF16)
+        here = a1_in.at[t, k, xc]
         for d in range(1, nxc):
-            to = lax.rem(xc + d, nxc)
-            remote(a1_out.at[t, k, lax.rem(to, 2)], a1_in.at[t, k, xc], send.at[t, k, S_A1], recv.at[t, k, S_A1],
-                   at_src(zh * nxc + to))
-
-    other = (1 - zh) * nxc + xc - core
+            remote(here, here, send.at[t, k, S_A1], recv.at[t, k, S_A1], at_src(zh * nxc + lax.rem(xc + d, nxc)))
 
     def stage_a2(t, k):
         wait_bytes(a1_in.at[t, k, pl.ds(0, nxc - 1)], recv.at[t, k, S_A1])
         total = a1_in[t, k, 0].astype(F32)
         for i in range(1, nxc):
             total += a1_in[t, k, i].astype(F32)
-        a2_in[t, k, zh * 2 + core, 0:half_rows] = total[0:half_rows].astype(BF16)
-        a2_in[t, k, zh * 2 + core, half_rows] = encode(decode(total[half_rows])).astype(BF16)
-        here = a2_in.at[t, k, zh * 2 + core]
-        for to in (other + core, other + 1 - core, src + 1 - 2 * core):
-            remote(here, here, send.at[t, k, S_A2], recv.at[t, k, S_A2], at_src(to))
+        a2_in[t, k, zh, 0:ny] = total[0:ny].astype(BF16)
+        a2_in[t, k, zh, ny] = encode(decode(total[ny])).astype(BF16)
+        here = a2_in.at[t, k, zh]
+        remote(here, here, send.at[t, k, S_A2], recv.at[t, k, S_A2], at_src((1 - zh) * nxc + xc))
 
     def stage_a3(t, k):
-        wait_bytes(a2_in.at[t, k, pl.ds(0, 3)], recv.at[t, k, S_A2])
-        totals = [a2_in[t, k, c].astype(F32) + a2_in[t, k, 2 + c].astype(F32) for c in range(2)]
-        vector = jnp.concatenate([total[0:half_rows] for total in totals], axis=0)
+        wait_bytes(a2_in.at[t, k, 0], recv.at[t, k, S_A2])
+        total = a2_in[t, k, 0].astype(F32) + a2_in[t, k, 1].astype(F32)
+        vector = total[0:ny]
         if t > 0:
-            squares = [decode(total[half_rows]) for total in totals]
-            alpha[k] = root(jnp.stack(unpack(squares[0]) + unpack(squares[1])), cols_total)
+            alpha[k] = root(unpack(decode(total[ny])), cols_total)
             wait_bytes(beta_sq.at[t, k, pl.ds(0, ny - 1)], recv.at[t, k, S_BETA])
             beta = root(beta_squares(t, k), rows_total)
             vector = vector / alpha[k] - alpha[k] * (uhat[k] / beta)
         uhat[k] = vector
-        scalars = encode(squares_of([vector])).astype(BF16)
         turned = swap(vector)
         left = jnp.concatenate([vector, jnp.where(is_re(turned.shape), turned, -turned)], axis=-1)
         left = left.reshape(ny * PART, 2 * rows_half).astype(BF16)
         for i in range(nq):
             q = by_distance(i, True)
             back = jnp.dot(left, gmat[q], preferred_element_type=F32)
-            b1_out[t, k, q, :, :, 0:width] = back.reshape(ny, PART, width).astype(BF16)
-            b1_out[t, k, q, :, :, width:] = scalars
+            b1_out[t, k, q] = back.reshape(ny, PART, width).astype(BF16)
             if i < nq - 1:
                 remote(b1_out.at[t, k, q, y], b1_in.at[t, k, slot], send.at[t, k, S_B1], recv.at[t, k, S_B1],
                        at_sta(zhalf * nq + q, y))
@@ -274,14 +261,35 @@
                 remote(b1_out.at[t, k, q, y_peer(d)], b1_in.at[t, k, slot], send.at[t, k, S_B1],
                        recv.at[t, k, S_B1], at_sta(zhalf * nq + q, y_peer(d)))
 
+            if i == 0:
+                by_out[t, k] = squares_of([vector])
+                for d in y_order:
+                    remote(by_out.at[t, k, y_peer(d)], by_in.at[t, k, y], send.at[t, k, S_BY], recv.at[t, k, S_BY],
+                           at_sta(z, y_peer(d)))
+
+    def stage_squares(t, k):
+        b1_in[t, k, slot] = b1_out[t, k, quad, y]
+        wait_bytes(by_in.at[t, k, pl.ds(0, ny - 1)], recv.at[t, k, S_BY])
+        squares = by_out[t, k, y]
+        for d in range(1, ny):
+            squares += by_in[t, k, y_peer(d)]
+        bq_in[t, k, quad] = squares
+        here = bq_in.at[t, k, quad]
+        for i in range(nq - 1):
+            remote(here, here, send.at[t, k, S_BQ], recv.at[t, k, S_BQ],
+                   at_sta(zhalf * nq + by_distance(i, True), y))
+
     def stage_b3(t, k):
-        b1_in[t, k, slot] = b1_out[t, k, quad, y]
+        wait_bytes(bq_in.at[t, k, pl.ds(0, nq - 1)], recv.at[t, k, S_BQ])
+        squares = bq_in[t, k, 0]
+        for i in range(1, nq):
+            squares += bq_in[t, k, i]
+        b3_out[t, k, :, width:] = encode(squares).astype(BF16)
         wait_bytes(b1_in.at[t, k, pl.ds(0, n_own - 1)], recv.at[t, k, S_B1])
         total = b1_in[t, k, 0].astype(F32)
         for i in range(1, n_own):
             total += b1_in[t, k, i].astype(F32)
-        b3_out[t, k, :, 0:width] = total[:, :width].astype(BF16)
-        b3_out[t, k, :, width:] = encode(decode(total[:, width:])).astype(BF16)
+        b3_out[t, k, :, 0:width] = total.astype(BF16)
         remote(b3_out.at[t, k], b3_in.at[t, k], send.at[t, k, S_B3], recv.at[t, k, S_B3],
                at_sta((1 - zhalf) * nq + quad, y))
 
@@ -360,6 +368,8 @@
             stage_a2(t, k)
         for k in range(groups):
             stage_a3(t, k)
+        for k in range(groups):
+            stage_squares(t, k)
         if t > 0:
             for k in range(groups):
                 rotate(k, root(beta_squares(t, k), rows_total))
@@ -370,7 +380,6 @@
 
     row = lax.broadcasted_iota(jnp.int32, (PART, LANES), 0)
     lane = lax.broadcasted_iota(jnp.int32, (PART, LANES), 1)
-    seg = LANES // ny
     squares = jnp.zeros((PART, LANES), F32)
     betas = []
     for k in range(groups):
@@ -432,7 +441,9 @@
         wait_bytes(fs1.at[k, pl.ds(0, ny * nq - 1)], send.at[ITERS, k, 0])
         for t in range(ITERS):
             wait_bytes(a1_in.at[t, k, pl.ds(0, nxc - 1)], send.at[t, k, S_A1])
-            wait_bytes(a2_in.at[t, k, pl.ds(0, 3)], send.at[t, k, S_A2])
+            wait_bytes(a2_in.at[t, k, 0], send.at[t, k, S_A2])
+            wait_bytes(by_in.at[t, k, pl.ds(0, ny - 1)], send.at[t, k, S_BY])
+            wait_bytes(bq_in.at[t, k, pl.ds(0, nq - 1)], send.at[t, k, S_BQ])
             wait_bytes(vall.at[t, k, pl.ds(0, blocks_in(t))], send.at[t, k, S_V])
             wait_bytes(b1_in.at[t, k, pl.ds(0, n_own - 1)], send.at[t, k, S_B1])
             wait_bytes(b3_in.at[t, k], send.at[t, k, S_B3])
@@ -461,7 +472,6 @@
     args = list(args[:6]) + [a.reshape(1, n_events) for a in args[6:]]
     vmem = pl.BlockSpec(memory_space=pltpu.VMEM)
     hbm = pl.BlockSpec(memory_space=pltpu.HBM)
-    half = ny // 2
 
     def buf(*shape, kind=BF16):
         return pltpu.VMEM(shape, kind)
@@ -476,13 +486,15 @@
         buf(grid.nz, 2 * nq, width),
         buf(groups, nq, PART, width, kind=F32),
         buf(ITERS + 1, groups, ny * nq, PART, width),
-        buf(ITERS, groups, 2, half + 1, PART, LANES),
-        buf(ITERS, groups, grid.nxc, half + 1, PART, LANES),
-        buf(ITERS, groups, 4, half + 1, PART, LANES),
+        buf(ITERS, groups, grid.nxc, ny + 1, PART, LANES),
+        buf(ITERS, groups, grid.nzh, ny + 1, PART, LANES),
         buf(groups, ny * nq, PART, LANES, kind=F32),
         buf(grid.nzh * grid.nxc, PART, LANES, kind=F32),
-        buf(ITERS, groups, nq, ny, PART, padded),
-        buf(ITERS, groups, ny * nq, PART, padded),
+        buf(ITERS, groups, nq, ny, PART, width),
+        buf(ITERS, groups, ny * nq, PART, width),
+        buf(ITERS, groups, ny, PART, LANES, kind=F32),
+        buf(ITERS, groups, ny, PART, LANES, kind=F32),
+        buf(ITERS, groups, nq, PART, LANES, kind=F32),
         buf(ITERS, groups, PART, padded),
         buf(ITERS, groups, PART, padded),
         buf(ITERS, groups, ny, PART, LANES, kind=F32),
@@ -492,8 +504,8 @@
         pltpu.SemaphoreType.DMA((7 + 2 * nq,)),
         pltpu.SemaphoreType.DMA,
         pltpu.SemaphoreType.DMA,
-        pltpu.SemaphoreType.DMA((ITERS + 1, groups, 7)),
-        pltpu.SemaphoreType.DMA((ITERS + 1, groups, 7)),
+        pltpu.SemaphoreType.DMA((ITERS + 1, groups, 9)),
+        pltpu.SemaphoreType.DMA((ITERS + 1, groups, 9)),
     ]
     shapes = [station.shape, source.shape, source.shape, source.shape] + [(1, n_events)] * 3
     shapes = [jax.ShapeDtypeStruct(shape, F32) for shape in shapes]

time: 134 us -> 131 us (0.978)
  Pallas kernels: 133 us -> 130 us
    pallas_call x1, Pallas kernels: 132 us -> 129 us  [shards(): pl.pallas_call(functools.partial(kernel, grid, rows_total, cols_total), o...]
where the time goes in v5:
time: 131 us
  Pallas kernels  130 us (99%)
    pallas_call x1, Pallas kernels, shards(): pl.pallas_call(functools.partial(kernel, grid, rows_total, cols_total), o...  129 us

profile of v5, /device:TPU:1, one launch (start us, length us, event | category | flops | bytes accessed | tf_op | source)
XLA Modules:
  0.0 130.6 jit_solution(8020281419752587722)
XLA Ops:
  0.6 128.5 %lsqr.1 = (f32[2,2,128]{2,1,0:T(2,128)}, f32[2,1,2048]{2,1,0:T(1,128)}, f32[2,1,2048]{2,1,0:T(1,128)}, f32[2,1,2048]{2,1,0:T(1,128)}, f32[1,32]{1,0:T(1,128)}, /*index=5*/f32[1,32]{1,0:T(1,128)}, f32[1,32]{1,0:T(1,128)}) custom-call(bf16[128,2048]{1,0:T(8,128)(2,1)} %refs_0_.1, bf16[128,2048]{1,0:T(8,128)(2,1)} %refs_1_.1, f32[2,2,128]{2,1,0:T(2,128)} %refs_2_.1, ...), custom_call_target="tpu_custom_call" | custom-call | tf_op jit(solution)/shard_map/lsqr/pallas_call | solution.py:512
  129.2 1.5 %deliver.1 = (f32[2,2,128]{2,1,0:T(2,128)}, f32[2,1,2048]{2,1,0:T(1,128)}, f32[2,1,2048]{2,1,0:T(1,128)}, f32[2,1,2048]{2,1,0:T(1,128)}, f32[1,32]{1,0:T(1,128)}, /*index=5*/f32[1,32]{1,0:T(1,128)}, f32[1,32]{1,0:T(1,128)}) custom-call(f32[2,2,128]{2,1,0:T(2,128)} %get-tuple-element.21.refs_0_, f32[2,1,2048]{2,1,0:T(1,128)} %get-tuple-element.22.refs_1_, ...), custom_call_target="tpu_custom_call" | custom-call | tf_op jit(solution)/shard_map/deliver/pallas_call | solution.py:522

commit v6 on v5

--- a/solution.py
+++ b/solution.py
@@ -41,7 +41,7 @@
     width = source_ref.shape[-1] // nq
     rows_half = gmat.shape[1] // 2
     ratio = cols_total / rows_total
-    S_A1, S_A2, S_B1, S_B3, S_V, S_BETA, S_LAST, S_BY, S_BQ = range(9)
+    S_A1, S_A2, S_B3, S_BETA, S_LAST, S_BY, S_BQ, S_V, S_B1 = *range(8), 7 + nq
     n_own = ny * nq
 
     sta = lax.axis_index("sta")
@@ -158,17 +158,17 @@
             for p in range(2):
                 for q in range(nq):
                     first_rows[k, q, p * per + e : p * per + e + 1, :] = block[p * nq + q : p * nq + q + 1, :]
-        mine = pl.ds(y * nq, nq)
-        vall[0, k, mine] = first_rows[k].astype(BF16)
-        for d in y_order:
-            remote(vall.at[0, k, mine], vall.at[0, k, mine], send.at[0, k, S_V], recv.at[0, k, S_V],
-                   at_sta(z, y_peer(d)))
+        for q in range(nq):
+            vall[0, k, q * ny + y] = first_rows[k, q].astype(BF16)
+            here = vall.at[0, k, q * ny + y]
+            for d in y_order:
+                remote(here, here, send.at[0, k, S_V], recv.at[0, k, S_V + q], at_sta(z, y_peer(d)))
 
     def blocks_in(t):
         return n_own - (nq if t == 0 else 1)
 
     def columns(t, k, q):
-        return jnp.stack([vall[t, k, i * nq + q].astype(F32) for i in range(ny)])
+        return vall[t, k, pl.ds(q * ny, ny)].astype(F32)
 
     def beta_squares(t, k):
         return beta_sq[t, k]
@@ -197,14 +197,17 @@
 
     contract = (((1,), (1,)), ((), ()))
 
-    slot = y * nq + quad
+    slot = quad * ny + y
 
     def stage_a1(t, k):
-        wait_bytes(vall.at[t, k, pl.ds(0, blocks_in(t))], recv.at[t, k, S_V])
-        values = [columns(t, k, q) for q in range(nq)]
         product = jnp.zeros((ny * PART, 2 * rows_half), F32)
-        for q in range(nq):
-            left = values[q].reshape(ny * PART, width).astype(BF16)
+        values = []
+        for i in range(nq):
+            q = by_distance(i, False)
+            own_column = t == 0 or i == 0
+            wait_bytes(vall.at[t, k, pl.ds(0, ny - 1 if own_column else ny)], recv.at[t, k, S_V + q])
+            values.append(columns(t, k, q))
+            left = values[i].reshape(ny * PART, width).astype(BF16)
             product += lax.dot_general(left, gmat[q], contract, preferred_element_type=F32)
         product = product.reshape(ny, PART, 2 * rows_half)
         turned = swap(product[..., rows_half:])
@@ -220,7 +223,7 @@
                                  jnp.broadcast_to(station_ref[1, n : n + 1, :][None], shape))
                 image -= jnp.where(event == src * per_src + n, alpha[k] * both, 0.0)
         else:
-            scalars = encode(squares_of(values))
+            scalars = encode(squares_of([columns(t, k, q) for q in range(nq)]))
         a1_in[t, k, xc, 0:ny] = image.astype(BF16)
         a1_in[t, k, xc, ny] = pack(scalars).astype(BF16)
         here = a1_in.at[t, k, xc]
@@ -255,11 +258,11 @@
             back = jnp.dot(left, gmat[q], preferred_element_type=F32)
             b1_out[t, k, q] = back.reshape(ny, PART, width).astype(BF16)
             if i < nq - 1:
-                remote(b1_out.at[t, k, q, y], b1_in.at[t, k, slot], send.at[t, k, S_B1], recv.at[t, k, S_B1],
-                       at_sta(zhalf * nq + q, y))
+                remote(b1_out.at[t, k, q, y], b1_in.at[t, k, quad, y], send.at[t, k, S_B1],
+                       recv.at[t, k, S_B1 + quad], at_sta(zhalf * nq + q, y))
             for d in y_order:
-                remote(b1_out.at[t, k, q, y_peer(d)], b1_in.at[t, k, slot], send.at[t, k, S_B1],
-                       recv.at[t, k, S_B1], at_sta(zhalf * nq + q, y_peer(d)))
+                remote(b1_out.at[t, k, q, y_peer(d)], b1_in.at[t, k, quad, y], send.at[t, k, S_B1],
+                       recv.at[t, k, S_B1 + quad], at_sta(zhalf * nq + q, y_peer(d)))
 
             if i == 0:
                 by_out[t, k] = squares_of([vector])
@@ -268,7 +271,6 @@
                            at_sta(z, y_peer(d)))
 
     def stage_squares(t, k):
-        b1_in[t, k, slot] = b1_out[t, k, quad, y]
         wait_bytes(by_in.at[t, k, pl.ds(0, ny - 1)], recv.at[t, k, S_BY])
         squares = by_out[t, k, y]
         for d in range(1, ny):
@@ -285,10 +287,15 @@
         for i in range(1, nq):
             squares += bq_in[t, k, i]
         b3_out[t, k, :, width:] = encode(squares).astype(BF16)
-        wait_bytes(b1_in.at[t, k, pl.ds(0, n_own - 1)], recv.at[t, k, S_B1])
-        total = b1_in[t, k, 0].astype(F32)
-        for i in range(1, n_own):
-            total += b1_in[t, k, i].astype(F32)
+        total = b1_out[t, k, quad, y].astype(F32)
+        wait_bytes(b1_in.at[t, k, 0, pl.ds(0, ny - 1)], recv.at[t, k, S_B1 + quad])
+        for d in range(1, ny):
+            total += b1_in[t, k, quad, y_peer(d)].astype(F32)
+        for i in range(1, nq):
+            q = by_distance(i, False)
+            wait_bytes(b1_in.at[t, k, 0], recv.at[t, k, S_B1 + q])
+            for j in range(ny):
+                total += b1_in[t, k, q, j].astype(F32)
         b3_out[t, k, :, 0:width] = total.astype(BF16)
         remote(b3_out.at[t, k], b3_in.at[t, k], send.at[t, k, S_B3], recv.at[t, k, S_B3],
                at_sta((1 - zhalf) * nq + quad, y))
@@ -313,7 +320,7 @@
         vall[t + 1, k, slot] = after
         here = vall.at[t + 1, k, slot]
         if t < ITERS - 1:
-            to_half(here, send.at[t + 1, k, S_V], recv.at[t + 1, k, S_V])
+            to_half(here, send.at[t + 1, k, S_V], recv.at[t + 1, k, S_V + quad])
             beta_sq[t + 1, k, y] = squares
             for d in y_order:
                 remote(beta_sq.at[t + 1, k, y], beta_sq.at[t + 1, k, y], send.at[t + 1, k, S_BETA],
@@ -340,7 +347,7 @@
         phi[k] = sine * phi[k]
 
     def own_rows(t):
-        block = vall[t, mine_k, pl.ds(y * nq, nq)].astype(F32)
+        block = jnp.stack([vall[t, mine_k, q * ny + y].astype(F32) for q in range(nq)])
         row = lax.broadcasted_iota(jnp.int32, block.shape, 1)
         result = []
         for p in range(2):
@@ -386,16 +393,19 @@
         wait_bytes(fs1.at[k, pl.ds(0, ny * nq - 1)], recv.at[ITERS, k, 0])
         beta_rows = []
         for i in range(ny):
-            total = fs1[k, i * nq]
+            total = fs1[k, i]
             beta_rows.append(lanes(total[:, LANES // 2 : LANES // 2 + 1]))
             for q in range(1, nq):
-                total += fs1[k, i * nq + q]
+                total += fs1[k, q * ny + i]
             squares = jnp.where((lax.div(lane, seg) == i) & (lax.div(row, per) == k), lanes(total[:, 0:1]), squares)
         betas.append(root(jnp.stack(beta_rows), rows_total))
-    fs2[src] = squares
-    for d in range(1, n_src):
-        remote(fs2.at[src], fs2.at[src], send.at[ITERS, 0, 1], recv.at[ITERS, 0, 1],
-               at_src(lax.rem(src + d, n_src)))
+    high = squares.astype(BF16).astype(F32)
+    fs2[src] = jnp.where(lax.rem(lane, seg) < seg // 2, high, squares - high).astype(BF16)
+    for other in range(1, -1, -1):
+        for d in range(nxc):
+            if other or d:
+                remote(fs2.at[src], fs2.at[src], send.at[ITERS, 0, 1], recv.at[ITERS, 0, 1],
+                       at_src((1 - zh if other else zh) * nxc + lax.rem(xc + d, nxc)))
 
     for k in range(groups):
         unorm[k] = uhat[k] / betas[k]
@@ -411,13 +421,14 @@
     last_rows = own_rows(ITERS)
 
     wait_bytes(fs2.at[pl.ds(0, n_src - 1)], recv.at[ITERS, 0, 1])
-    squares = fs2[0]
+    squares = fs2[0].astype(F32)
     for i in range(1, n_src):
-        squares += fs2[i]
+        squares += fs2[i].astype(F32)
     for k in range(groups):
         kept = jnp.where(lax.div(row, per) == k, squares, 0.0)
         kept = kept + swap(kept)
-        alpha[k] = root(jnp.stack([lanes(kept[:, i * seg : i * seg + 1]) for i in range(ny)]), cols_total)
+        alpha[k] = root(jnp.stack([lanes(kept[:, i * seg : i * seg + 1] + kept[:, i * seg + seg // 2 : i * seg + seg // 2 + 1])
+                                   for i in range(ny)]), cols_total)
         rotate(k, betas[k])
     step(ITERS, last_rows)
 
@@ -445,7 +456,7 @@
             wait_bytes(by_in.at[t, k, pl.ds(0, ny - 1)], send.at[t, k, S_BY])
             wait_bytes(bq_in.at[t, k, pl.ds(0, nq - 1)], send.at[t, k, S_BQ])
             wait_bytes(vall.at[t, k, pl.ds(0, blocks_in(t))], send.at[t, k, S_V])
-            wait_bytes(b1_in.at[t, k, pl.ds(0, n_own - 1)], send.at[t, k, S_B1])
+            wait_bytes(vall.at[t, k, pl.ds(0, n_own - 1)], send.at[t, k, S_B1])
             wait_bytes(b3_in.at[t, k], send.at[t, k, S_B3])
             if t > 0:
                 wait_bytes(beta_sq.at[t, k, pl.ds(0, ny - 1)], send.at[t, k, S_BETA])
@@ -489,9 +500,9 @@
         buf(ITERS, groups, grid.nxc, ny + 1, PART, LANES),
         buf(ITERS, groups, grid.nzh, ny + 1, PART, LANES),
         buf(groups, ny * nq, PART, LANES, kind=F32),
-        buf(grid.nzh * grid.nxc, PART, LANES, kind=F32),
+        buf(grid.nzh * grid.nxc, PART, LANES),
         buf(ITERS, groups, nq, ny, PART, width),
-        buf(ITERS, groups, ny * nq, PART, width),
+        buf(ITERS, groups, nq, ny, PART, width),
         buf(ITERS, groups, ny, PART, LANES, kind=F32),
         buf(ITERS, groups, ny, PART, LANES, kind=F32),
         buf(ITERS, groups, nq, PART, LANES, kind=F32),
@@ -504,8 +515,8 @@
         pltpu.SemaphoreType.DMA((7 + 2 * nq,)),
         pltpu.SemaphoreType.DMA,
         pltpu.SemaphoreType.DMA,
-        pltpu.SemaphoreType.DMA((ITERS + 1, groups, 9)),
-        pltpu.SemaphoreType.DMA((ITERS + 1, groups, 9)),
+        pltpu.SemaphoreType.DMA((ITERS + 1, groups, 7 + 2 * nq)),
+        pltpu.SemaphoreType.DMA((ITERS + 1, groups, 7 + 2 * nq)),
     ]
     shapes = [station.shape, source.shape, source.shape, source.shape] + [(1, n_events)] * 3
     shapes = [jax.ShapeDtypeStruct(shape, F32) for shape in shapes]

time: 131 us -> 131 us (level)
  no operation moved by 1% of the time
where the time goes in v6:
time: 131 us
  Pallas kernels  130 us (99%)
    pallas_call x1, Pallas kernels, shards(): pl.pallas_call(functools.partial(kernel, grid, rows_total, cols_total), o...  129 us

profile of v6, /device:TPU:1, one launch (start us, length us, event | category | flops | bytes accessed | tf_op | source)
XLA Modules:
  0.0 131.0 jit_solution(17673322643471452163)
XLA Ops:
  0.6 128.9 %lsqr.1 = (f32[2,2,128]{2,1,0:T(2,128)}, f32[2,1,2048]{2,1,0:T(1,128)}, f32[2,1,2048]{2,1,0:T(1,128)}, f32[2,1,2048]{2,1,0:T(1,128)}, f32[1,32]{1,0:T(1,128)}, /*index=5*/f32[1,32]{1,0:T(1,128)}, f32[1,32]{1,0:T(1,128)}) custom-call(bf16[128,2048]{1,0:T(8,128)(2,1)} %refs_0_.1, bf16[128,2048]{1,0:T(8,128)(2,1)} %refs_1_.1, f32[2,2,128]{2,1,0:T(2,128)} %refs_2_.1, ...), custom_call_target="tpu_custom_call" | custom-call | tf_op jit(solution)/shard_map/lsqr/pallas_call | solution.py:523
  129.6 1.5 %deliver.1 = (f32[2,2,128]{2,1,0:T(2,128)}, f32[2,1,2048]{2,1,0:T(1,128)}, f32[2,1,2048]{2,1,0:T(1,128)}, f32[2,1,2048]{2,1,0:T(1,128)}, f32[1,32]{1,0:T(1,128)}, /*index=5*/f32[1,32]{1,0:T(1,128)}, f32[1,32]{1,0:T(1,128)}) custom-call(f32[2,2,128]{2,1,0:T(2,128)} %get-tuple-element.21.refs_0_, f32[2,1,2048]{2,1,0:T(1,128)} %get-tuple-element.22.refs_1_, ...), custom_call_target="tpu_custom_call" | custom-call | tf_op jit(solution)/shard_map/deliver/pallas_call | solution.py:533

commit v7 on v6

--- a/solution.py
+++ b/solution.py
@@ -34,7 +34,7 @@
      station_out, source_out, search_out, sol_out, alpha_out, rho_out, phi_out,
      station_ref, source_ref, alpha_ref, rho_ref, phi_ref,
      gmat, first, first_rows, vall, a1_in, a2_in, fs1, fs2,
-     b1_out, b1_in, by_out, by_in, bq_in, b3_out, b3_in, beta_sq,
+     b1_out, b1_in, by_in, bq_in, b3_out, b3_in, beta_sq,
      uhat, unorm, coef, load_sem, first_send, first_recv, send, recv) = refs
     ny, nq, nxc, groups, per = grid.ny, grid.nq, grid.nxc, grid.groups, grid.per
     n_src = grid.nzh * nxc
@@ -250,6 +250,11 @@
             beta = root(beta_squares(t, k), rows_total)
             vector = vector / alpha[k] - alpha[k] * (uhat[k] / beta)
         uhat[k] = vector
+        bq_in[t, k, quad] = pack(squares_of([vector]))
+        here = bq_in.at[t, k, quad]
+        for i in range(nq - 1):
+            remote(here, here, send.at[t, k, S_BQ], recv.at[t, k, S_BQ],
+                   at_sta(zhalf * nq + by_distance(i, True), y))
         turned = swap(vector)
         left = jnp.concatenate([vector, jnp.where(is_re(turned.shape), turned, -turned)], axis=-1)
         left = left.reshape(ny * PART, 2 * rows_half).astype(BF16)
@@ -264,28 +269,25 @@
                 remote(b1_out.at[t, k, q, y_peer(d)], b1_in.at[t, k, quad, y], send.at[t, k, S_B1],
                        recv.at[t, k, S_B1 + quad], at_sta(zhalf * nq + q, y_peer(d)))
 
-            if i == 0:
-                by_out[t, k] = squares_of([vector])
-                for d in y_order:
-                    remote(by_out.at[t, k, y_peer(d)], by_in.at[t, k, y], send.at[t, k, S_BY], recv.at[t, k, S_BY],
-                           at_sta(z, y_peer(d)))
 
     def stage_squares(t, k):
-        wait_bytes(by_in.at[t, k, pl.ds(0, ny - 1)], recv.at[t, k, S_BY])
-        squares = by_out[t, k, y]
-        for d in range(1, ny):
-            squares += by_in[t, k, y_peer(d)]
-        bq_in[t, k, quad] = squares
-        here = bq_in.at[t, k, quad]
-        for i in range(nq - 1):
-            remote(here, here, send.at[t, k, S_BQ], recv.at[t, k, S_BQ],
-                   at_sta(zhalf * nq + by_distance(i, True), y))
-
-    def stage_b3(t, k):
         wait_bytes(bq_in.at[t, k, pl.ds(0, nq - 1)], recv.at[t, k, S_BQ])
         squares = bq_in[t, k, 0]
         for i in range(1, nq):
             squares += bq_in[t, k, i]
+        by_in[t, k, y] = squares
+        here = by_in.at[t, k, y]
+        for d in y_order:
+            remote(here, here, send.at[t, k, S_BY], recv.at[t, k, S_BY], at_sta(z, y_peer(d)))
+
+    def stage_b3(t, k):
+        wait_bytes(by_in.at[t, k, pl.ds(0, ny - 1)], recv.at[t, k, S_BY])
+        total = by_in[t, k, 0]
+        for i in range(1, ny):
+            total += by_in[t, k, i]
+        squares = jnp.zeros((PART, LANES), F32)
+        for i in range(ny):
+            squares = jnp.where(y == i, lanes(total[:, i * seg : i * seg + 1]), squares)
         b3_out[t, k, :, width:] = encode(squares).astype(BF16)
         total = b1_out[t, k, quad, y].astype(F32)
         wait_bytes(b1_in.at[t, k, 0, pl.ds(0, ny - 1)], recv.at[t, k, S_B1 + quad])
@@ -503,7 +505,6 @@
         buf(grid.nzh * grid.nxc, PART, LANES),
         buf(ITERS, groups, nq, ny, PART, width),
         buf(ITERS, groups, nq, ny, PART, width),
-        buf(ITERS, groups, ny, PART, LANES, kind=F32),
         buf(ITERS, groups, ny, PART, LANES, kind=F32),
         buf(ITERS, groups, nq, PART, LANES, kind=F32),
         buf(ITERS, groups, PART, padded),

time: 131 us -> 133 us (1.015)
  Pallas kernels: 130 us -> 133 us
    pallas_call x1, Pallas kernels: 129 us -> 131 us  [shards(): pl.pallas_call(functools.partial(kernel, grid, rows_total, cols_total), o...]
where the time goes in v7:
time: 133 us
  Pallas kernels  133 us (100%)
    pallas_call x1, Pallas kernels, shards(): pl.pallas_call(functools.partial(kernel, grid, rows_total, cols_total), o...  131 us

profile of v7, /device:TPU:1, one launch (start us, length us, event | category | flops | bytes accessed | tf_op | source)
XLA Modules:
  0.0 133.2 jit_solution(11380040110487531543)
XLA Ops:
  0.6 131.1 %lsqr.1 = (f32[2,2,128]{2,1,0:T(2,128)}, f32[2,1,2048]{2,1,0:T(1,128)}, f32[2,1,2048]{2,1,0:T(1,128)}, f32[2,1,2048]{2,1,0:T(1,128)}, f32[1,32]{1,0:T(1,128)}, /*index=5*/f32[1,32]{1,0:T(1,128)}, f32[1,32]{1,0:T(1,128)}) custom-call(bf16[128,2048]{1,0:T(8,128)(2,1)} %refs_0_.1, bf16[128,2048]{1,0:T(8,128)(2,1)} %refs_1_.1, f32[2,2,128]{2,1,0:T(2,128)} %refs_2_.1, ...), custom_call_target="tpu_custom_call" | custom-call | tf_op jit(solution)/shard_map/lsqr/pallas_call | solution.py:524
  131.8 1.5 %deliver.1 = (f32[2,2,128]{2,1,0:T(2,128)}, f32[2,1,2048]{2,1,0:T(1,128)}, f32[2,1,2048]{2,1,0:T(1,128)}, f32[2,1,2048]{2,1,0:T(1,128)}, f32[1,32]{1,0:T(1,128)}, /*index=5*/f32[1,32]{1,0:T(1,128)}, f32[1,32]{1,0:T(1,128)}) custom-call(f32[2,2,128]{2,1,0:T(2,128)} %get-tuple-element.21.refs_0_, f32[2,1,2048]{2,1,0:T(1,128)} %get-tuple-element.22.refs_1_, ...), custom_call_target="tpu_custom_call" | custom-call | tf_op jit(solution)/shard_map/deliver/pallas_call | solution.py:534

commit v8 on v6

--- a/solution.py
+++ b/solution.py
@@ -275,18 +275,12 @@
         squares = by_out[t, k, y]
         for d in range(1, ny):
             squares += by_in[t, k, y_peer(d)]
-        bq_in[t, k, quad] = squares
-        here = bq_in.at[t, k, quad]
-        for i in range(nq - 1):
-            remote(here, here, send.at[t, k, S_BQ], recv.at[t, k, S_BQ],
-                   at_sta(zhalf * nq + by_distance(i, True), y))
+        bq_in[t, k, z] = encode(squares).astype(BF16)
+        here = bq_in.at[t, k, z]
+        for d in range(1, grid.nz):
+            remote(here, here, send.at[t, k, S_BQ], recv.at[t, k, S_BQ], at_sta(lax.rem(z + d, grid.nz), y))
 
     def stage_b3(t, k):
-        wait_bytes(bq_in.at[t, k, pl.ds(0, nq - 1)], recv.at[t, k, S_BQ])
-        squares = bq_in[t, k, 0]
-        for i in range(1, nq):
-            squares += bq_in[t, k, i]
-        b3_out[t, k, :, width:] = encode(squares).astype(BF16)
         total = b1_out[t, k, quad, y].astype(F32)
         wait_bytes(b1_in.at[t, k, 0, pl.ds(0, ny - 1)], recv.at[t, k, S_B1 + quad])
         for d in range(1, ny):
@@ -296,7 +290,7 @@
             wait_bytes(b1_in.at[t, k, 0], recv.at[t, k, S_B1 + q])
             for j in range(ny):
                 total += b1_in[t, k, q, j].astype(F32)
-        b3_out[t, k, :, 0:width] = total.astype(BF16)
+        b3_out[t, k] = total.astype(BF16)
         remote(b3_out.at[t, k], b3_in.at[t, k], send.at[t, k, S_B3], recv.at[t, k, S_B3],
                at_sta((1 - zhalf) * nq + quad, y))
 
@@ -313,9 +307,13 @@
             before = before / coef[k, 0, y][:, 0:1]
         wait_bytes(b3_in.at[t, k], recv.at[t, k, S_B3])
         total = b3_out[t, k].astype(F32) + b3_in[t, k].astype(F32)
-        squares = decode(total[:, width:])
+        wait_bytes(bq_in.at[t, k, pl.ds(0, grid.nz - 1)], recv.at[t, k, S_BQ])
+        squares = bq_in[t, k, 0].astype(F32)
+        for i in range(1, grid.nz):
+            squares += bq_in[t, k, i].astype(F32)
+        squares = decode(squares)
         beta = root(squares, rows_total)[:, 0:1]
-        after = total[:, :width] * (ratio / beta) - beta * before
+        after = total * (ratio / beta) - beta * before
         after = after.astype(BF16)
         vall[t + 1, k, slot] = after
         here = vall.at[t + 1, k, slot]
@@ -454,7 +452,7 @@
             wait_bytes(a1_in.at[t, k, pl.ds(0, nxc - 1)], send.at[t, k, S_A1])
             wait_bytes(a2_in.at[t, k, 0], send.at[t, k, S_A2])
             wait_bytes(by_in.at[t, k, pl.ds(0, ny - 1)], send.at[t, k, S_BY])
-            wait_bytes(bq_in.at[t, k, pl.ds(0, nq - 1)], send.at[t, k, S_BQ])
+            wait_bytes(bq_in.at[t, k, pl.ds(0, grid.nz - 1)], send.at[t, k, S_BQ])
             wait_bytes(vall.at[t, k, pl.ds(0, blocks_in(t))], send.at[t, k, S_V])
             wait_bytes(vall.at[t, k, pl.ds(0, n_own - 1)], send.at[t, k, S_B1])
             wait_bytes(b3_in.at[t, k], send.at[t, k, S_B3])
@@ -478,7 +476,6 @@
     cols_total = green_real.shape[1] * lax.axis_size("src")
     ny, nq, groups = grid.ny, grid.nq, grid.groups
     width = green_real.shape[1] // nq
-    padded = width + LANES
     n_events = args[6].shape[0]
     args = list(args[:6]) + [a.reshape(1, n_events) for a in args[6:]]
     vmem = pl.BlockSpec(memory_space=pltpu.VMEM)
@@ -505,9 +502,9 @@
         buf(ITERS, groups, nq, ny, PART, width),
         buf(ITERS, groups, ny, PART, LANES, kind=F32),
         buf(ITERS, groups, ny, PART, LANES, kind=F32),
-        buf(ITERS, groups, nq, PART, LANES, kind=F32),
-        buf(ITERS, groups, PART, padded),
-        buf(ITERS, groups, PART, padded),
+        buf(ITERS, groups, grid.nz, PART, LANES),
+        buf(ITERS, groups, PART, width),
+        buf(ITERS, groups, PART, width),
         buf(ITERS, groups, ny, PART, LANES, kind=F32),
         buf(groups, ny, PART, rows, kind=F32),
         buf(groups, ny, PART, rows, kind=F32),

time: 131 us -> 129 us (0.985)
  Pallas kernels: 130 us -> 128 us
    pallas_call x1, Pallas kernels: 129 us -> 127 us  [shards(): pl.pallas_call(functools.partial(kernel, grid, rows_total, cols_total), o...]
where the time goes in v8:
time: 129 us
  Pallas kernels  128 us (99%)
    pallas_call x1, Pallas kernels, shards(): pl.pallas_call(functools.partial(kernel, grid, rows_total, cols_total), o...  127 us

profile of v8, /device:TPU:1, one launch (start us, length us, event | category | flops | bytes accessed | tf_op | source)
XLA Modules:
  0.0 128.9 jit_solution(4264176052908409187)
XLA Ops:
  0.6 126.8 %lsqr.1 = (f32[2,2,128]{2,1,0:T(2,128)}, f32[2,1,2048]{2,1,0:T(1,128)}, f32[2,1,2048]{2,1,0:T(1,128)}, f32[2,1,2048]{2,1,0:T(1,128)}, f32[1,32]{1,0:T(1,128)}, /*index=5*/f32[1,32]{1,0:T(1,128)}, f32[1,32]{1,0:T(1,128)}) custom-call(bf16[128,2048]{1,0:T(8,128)(2,1)} %refs_0_.1, bf16[128,2048]{1,0:T(8,128)(2,1)} %refs_1_.1, f32[2,2,128]{2,1,0:T(2,128)} %refs_2_.1, ...), custom_call_target="tpu_custom_call" | custom-call | tf_op jit(solution)/shard_map/lsqr/pallas_call | solution.py:520
  127.5 1.5 %deliver.1 = (f32[2,2,128]{2,1,0:T(2,128)}, f32[2,1,2048]{2,1,0:T(1,128)}, f32[2,1,2048]{2,1,0:T(1,128)}, f32[2,1,2048]{2,1,0:T(1,128)}, f32[1,32]{1,0:T(1,128)}, /*index=5*/f32[1,32]{1,0:T(1,128)}, f32[1,32]{1,0:T(1,128)}) custom-call(f32[2,2,128]{2,1,0:T(2,128)} %get-tuple-element.21.refs_0_, f32[2,1,2048]{2,1,0:T(1,128)} %get-tuple-element.22.refs_1_, ...), custom_call_target="tpu_custom_call" | custom-call | tf_op jit(solution)/shard_map/deliver/pallas_call | solution.py:530
